TPU v7x, 1024 devices: a whole 4x8x16 slice. The times are simulated.
1024 devices in a mesh: ctx: 64 (over x, z_lo, core), tp: 16 (over y, z_hi).
Axes of the slice: x: 4, y: 8, z: 16 (z_hi: 2, z_lo: 8; z = z_hi * 8 + z_lo), core: 2. Of those that a mesh axis runs over, the one named last changes fastest.
Arguments:
- query_in: bfloat16 [8192, 4096], P('ctx', 'tp'), may hold values from -6 to 6
- key_in: bfloat16 [8192, 4096], P('ctx', 'tp'), may hold values from -6 to 6
- value_in: bfloat16 [8192, 4096], P('ctx', 'tp'), may hold values from -6 to 6
- long_filter: bfloat16 [8192, 4096], P('ctx', 'tp'), may hold values from -1.1 to 1.1
- short_taps: bfloat16 [3, 3, 4096], P(None, None, 'tp'), may hold values from -3.5 to 3.5
- out_grad: bfloat16 [8192, 4096], P('ctx', 'tp'), may hold values from -6 to 6
Outputs:
- output: bfloat16 [8192, 4096], P('ctx', 'tp')
- query_grad: bfloat16 [8192, 4096], P('ctx', 'tp')
- key_grad: bfloat16 [8192, 4096], P('ctx', 'tp')
- value_grad: bfloat16 [8192, 4096], P('ctx', 'tp')
- filter_grad: float32 [8192, 4096], P('ctx', 'tp')
- taps_grad: float32 [3, 3, 4096], P(None, None, 'tp')
All inputs are finite; a program needn't handle non-finite values.
Results may differ from a plain program's by a relative error of at most 0.001.
Values may be sent and summed in bfloat16 or wider, within the bound.
A program may use at most 64 MiB of HBM per device.

v0:
```python
from functools import partial
import math

import jax
import jax.numpy as jnp
from jax import lax
from jax.sharding import PartitionSpec as P

HIGHEST_PREC = lax.Precision.HIGHEST
TWO_PI = 2.0 * math.pi


def passed_along(block, axis, distance):
    devices = range(lax.axis_size(axis))
    route = [(i - distance, i) for i in devices if i - distance in devices]
    return lax.ppermute(block, axis, route)


def phase_pair(count_a, count_b, period, direction):
    product = (
        jnp.arange(count_a, dtype=jnp.int32)[:, None]
        * jnp.arange(count_b, dtype=jnp.int32)[None, :]
    )
    phase_angle = direction * TWO_PI / period * (product % period).astype(jnp.float32)
    return (jnp.cos(phase_angle), jnp.sin(phase_angle))


def rotate_pair(real_part, imag_part, cosine, sine_part):
    return (real_part * cosine - imag_part * sine_part, real_part * sine_part + imag_part * cosine)


def times_pair(first_pair, second_pair, conj_second):
    factor = -1.0 if conj_second else 1.0
    real_part = first_pair[0] * second_pair[0] - factor * first_pair[1] * second_pair[1]
    imag_part = first_pair[1] * second_pair[0] + factor * first_pair[0] * second_pair[1]
    return (real_part, imag_part)


def unpack_fields(spectrum, comp_axis, field_axis):
    collected = []
    for partner_rank in range(spectrum.shape[field_axis]):
        single = lax.index_in_dim(spectrum, partner_rank, field_axis, keepdims=True)
        collected.append(
            (
                lax.index_in_dim(single, 0, comp_axis, keepdims=True),
                lax.index_in_dim(single, 1, comp_axis, keepdims=True),
            )
        )
    return collected


def pack_fields(pairs, comp_axis, field_axis):
    return jnp.concatenate(
        [jnp.concatenate([real_part, imag_part], axis=comp_axis) for real_part, imag_part in pairs],
        axis=field_axis,
    )


def spread_forward(regroup, fields):
    row_count, field_count, channels = fields.shape
    part_count = lax.axis_size("ctx")
    block_rows = row_count // part_count
    length = 2 * part_count * row_count
    my_index = lax.axis_index("ctx")
    gathered = regroup(fields.reshape(part_count, 1, block_rows, field_count, channels))
    cosine, sine_part = phase_pair(2 * part_count, part_count, 2 * part_count, -1.0)
    first_table = jnp.stack([cosine, sine_part], axis=1)
    first_pass = jnp.einsum("kda,arfc->kdrfc", first_table, gathered, precision=HIGHEST_PREC)
    row_index = my_index * block_rows + jnp.arange(block_rows, dtype=jnp.int32)
    twist_index = jnp.arange(2 * part_count, dtype=jnp.int32)[:, None] * row_index[None, :] % length
    phase_angle = -TWO_PI / length * twist_index.astype(jnp.float32)
    cos_twist = jnp.cos(phase_angle)[:, :, None, None]
    sin_twist = jnp.sin(phase_angle)[:, :, None, None]
    real_part, imag_part = rotate_pair(first_pass[:, 0], first_pass[:, 1], cos_twist, sin_twist)
    turned = jnp.stack([real_part, imag_part], axis=1)
    arrived = regroup(turned.reshape(part_count, 1, 2, 2, block_rows, field_count, channels))
    cosine, sine_part = phase_pair(row_count, row_count, row_count, -1.0)
    second_table = jnp.stack(
        [jnp.stack([cosine, sine_part], axis=-1), jnp.stack([-sine_part, cosine], axis=-1)], axis=0
    )
    second_table = second_table.reshape(2, part_count, block_rows, row_count, 2)
    return jnp.einsum("pqsrfc,sprkd->qkdfc", arrived, second_table, precision=HIGHEST_PREC)


def spread_inverse(regroup, spectrum):
    pair_count, row_count, _, field_count, channels = spectrum.shape
    part_count = lax.axis_size("ctx")
    block_rows = row_count // part_count
    length = 2 * part_count * row_count
    my_index = lax.axis_index("ctx")
    cosine, sine_part = phase_pair(row_count, row_count, row_count, 1.0)
    second_table = jnp.stack(
        [jnp.stack([cosine, sine_part], axis=-1), jnp.stack([-sine_part, cosine], axis=-1)], axis=0
    )
    second_table = second_table.reshape(2, row_count, part_count, block_rows, 2)
    row_parts = jnp.einsum("qkdfc,dkprs->pqsrfc", spectrum, second_table, precision=HIGHEST_PREC)
    freq_index = my_index * pair_count + jnp.arange(pair_count, dtype=jnp.int32)
    twist_index = freq_index[:, None] * jnp.arange(row_count, dtype=jnp.int32)[None, :] % length
    phase_angle = TWO_PI / length * twist_index.astype(jnp.float32)
    cos_twist = (
        jnp.cos(phase_angle)
        .reshape(pair_count, part_count, block_rows)
        .transpose(1, 0, 2)[:, :, :, None, None]
    )
    sin_twist = (
        jnp.sin(phase_angle)
        .reshape(pair_count, part_count, block_rows)
        .transpose(1, 0, 2)[:, :, :, None, None]
    )
    real_part, imag_part = rotate_pair(row_parts[:, :, 0], row_parts[:, :, 1], cos_twist, sin_twist)
    turned = jnp.stack([real_part, imag_part], axis=2)
    arrived = regroup(
        turned.reshape(part_count, 1, pair_count, 2, block_rows, field_count, channels)
    )
    cosine, sine_part = phase_pair(2 * part_count, part_count, 2 * part_count, 1.0)
    first_table = (jnp.stack([cosine, -sine_part], axis=1) / length).reshape(
        part_count, pair_count, 2, part_count
    )
    values = jnp.einsum("pqsrfc,pqsa->arfc", arrived, first_table, precision=HIGHEST_PREC)
    returned = regroup(values.reshape(part_count, 1, block_rows, field_count, channels))
    return returned.reshape(row_count, field_count, channels)


def local(query_in, key_in, value_in, long_filter, short_taps, out_grad):
    row_count = query_in.shape[0]
    tap_count = short_taps.shape[1]
    margin = tap_count - 1
    part_count = lax.axis_size("ctx")

    def regroup(blocks):
        return lax.all_to_all(blocks, "ctx", split_axis=0, concat_axis=1, tiled=True)[0]

    to_freq = partial(spread_forward, regroup)
    from_freq = partial(spread_inverse, regroup)
    comp_axis = 2
    field_axis = 3
    inputs = jnp.stack([query_in, key_in, value_in])
    earlier = passed_along(inputs[:, row_count - margin :], "ctx", 1)
    extended = jnp.concatenate([earlier, inputs], axis=1).astype(jnp.float32)
    tap_gain = short_taps.astype(jnp.float32)
    filtered = tap_gain[:, 0, None, :] * extended[:, margin:]
    for offset in range(1, tap_count):
        filtered = (
            filtered
            + tap_gain[:, offset, None, :]
            * extended[:, margin - offset : margin - offset + row_count]
        )
    query_filt = filtered[0]
    key_filt = filtered[1]
    value_filt = filtered[2]
    mixed_in = key_filt * value_filt
    spectra = to_freq(jnp.stack([mixed_in, long_filter.astype(jnp.float32)], axis=1))
    mixed_spec, filter_spec = unpack_fields(spectra, comp_axis, field_axis)
    convolved = from_freq(
        pack_fields([times_pair(mixed_spec, filter_spec, False)], comp_axis, field_axis)
    )[:, 0]
    output = (query_filt * convolved).astype(jnp.bfloat16)
    grad_in = out_grad.astype(jnp.float32)
    gate_grad = grad_in * convolved
    conv_grad = grad_in * query_filt
    grad_spec = unpack_fields(to_freq(conv_grad[:, None, :]), comp_axis, field_axis)[0]
    returned = from_freq(
        pack_fields(
            [times_pair(grad_spec, filter_spec, True), times_pair(grad_spec, mixed_spec, True)],
            comp_axis,
            field_axis,
        )
    )
    grad_scale = 1.0 / math.sqrt(part_count * row_count)
    mixed_grad = returned[:, 0]
    filter_grad = returned[:, 1] * grad_scale
    grad_stack = jnp.stack([gate_grad, mixed_grad * value_filt, mixed_grad * key_filt])
    later_rows = passed_along(grad_stack[:, :margin], "ctx", -1)
    padded_grad = jnp.concatenate([grad_stack, later_rows], axis=1)
    input_grads = tap_gain[:, 0, None, :] * grad_stack
    for offset in range(1, tap_count):
        input_grads = (
            input_grads + tap_gain[:, offset, None, :] * padded_grad[:, offset : offset + row_count]
        )
    partial_taps = jnp.stack(
        [
            jnp.sum(grad_stack * extended[:, margin - offset : margin - offset + row_count], axis=1)
            for offset in range(tap_count)
        ],
        axis=1,
    )
    taps_grad = lax.psum(partial_taps, "ctx") * grad_scale
    return (
        output,
        input_grads[0].astype(jnp.bfloat16),
        input_grads[1].astype(jnp.bfloat16),
        input_grads[2].astype(jnp.bfloat16),
        filter_grad,
        taps_grad,
    )


def solution(mesh):
    placed = (
        P("ctx", "tp"),
        P("ctx", "tp"),
        P("ctx", "tp"),
        P("ctx", "tp"),
        P(None, None, "tp"),
        P("ctx", "tp"),
    )
    return jax.shard_map(
        local,
        mesh=mesh,
        in_specs=placed,
        out_specs=(
            P("ctx", "tp"),
            P("ctx", "tp"),
            P("ctx", "tp"),
            P("ctx", "tp"),
            P("ctx", "tp"),
            P(None, None, "tp"),
        ),
        check_vma=False,
    )
```

profile of v0, /device:TPU:1, one launch (start us, length us, event | category | flops | bytes accessed | tf_op | source)
XLA Modules:
  0.0 741.8 jit_solution(5071711737848820669)
XLA Ops:
  0.7 0.8 pad_maximum_fusion.9
  1.4 5.4 collective-permute-start
  7.0 10.5 %collective-permute-done = bf16[3,2,256]{2,1,0:T(2,128)(2,1)S(1)} collective-permute-done((bf16[3,2,256]{2,1,0:T(2,128)(2,1)S(1)}, bf16[3,2,256]{2,1,0:T(2,128)(2,1)S(1)}, u32[]{:S(2)}, u32[]{:S(2)}) %collective-permute-start) | collective-permute-done | bytes 3104 | tf_op jit(solution)/shard_map/ppermute | solution.py:16
  17.8 0.2 pad_maximum_fusion.4
  18.1 0.9 copy.36
  19.0 9.1 %all-to-all-start = ((f32[64,1,2,2,256]{4,3,2,1,0:T(2,128)}), f32[64,1,2,2,256]{4,3,2,1,0:T(2,128)S(1)}, u32[]{:S(2)}, u32[]{:S(2)}) async-start(f32[64,1,2,2,256]{4,3,2,1,0:T(2,128)} %copy.36), calls=%async_computation | async-start | bytes 524288 | tf_op jit(solution)/shard_map/all_to_all | solution.py:131
  28.3 19.0 %all-to-all-done = f32[64,1,2,2,256]{4,3,2,1,0:T(2,128)S(1)} async-done(((f32[64,1,2,2,256]{4,3,2,1,0:T(2,128)}), f32[64,1,2,2,256]{4,3,2,1,0:T(2,128)S(1)}, u32[]{:S(2)}, u32[]{:S(2)}) %all-to-all-start) | async-done | bytes 262176 | tf_op jit(solution)/shard_map/all_to_all | solution.py:131
  47.3 1.0 fusion.23
  48.6 0.3 stack.73
  48.9 0.5 copy.38
  49.4 0.3 stack.74
  49.7 0.5 copy.39
  50.3 1.9 pad_maximum_fusion
  52.2 6.9 all-to-all-start.1
  59.3 0.3 fusion.60
  59.6 0.3 fusion.62
  60.0 50.4 %all-to-all-done.1 = f32[64,1,2,2,2,2,256]{6,3,4,5,2,1,0:T(2,128)S(1)} async-done(((f32[64,1,2,2,2,2,256]{6,3,4,5,2,1,0:T(2,128)}), f32[64,1,2,2,2,2,256]{6,3,4,5,2,1,0:T(2,128)S(1)}, u32[]{:S(2)}, u32[]{:S(2)}) %all-to-all-start.1) | async-done | bytes 1048608 | tf_op jit(solution)/shard_map/all_to_all | solution.py:131
  110.5 1.6 convolution_bitcast_fusion.1
  112.2 0.6 convolution_bitcast_fusion.2
  113.0 1.2 copy.42
  114.2 8.1 %all-to-all-start.2 = ((f32[64,1,2,2,2,1,256]{6,2,3,4,5,1,0:T(2,128)}), f32[64,1,2,2,2,1,256]{6,2,3,4,5,1,0:T(2,128)S(1)}, u32[]{:S(2)}, u32[]{:S(2)}) async-start(f32[64,1,2,2,2,1,256]{6,2,3,4,5,1,0:T(2,128)} %copy.42), calls=%async_computation.2 | async-start | bytes 1048576 | tf_op jit(solution)/shard_map/all_to_all | solution.py:131
  122.3 0.3 fusion.64
  122.6 29.3 %all-to-all-done.2 = f32[64,1,2,2,2,1,256]{6,2,3,4,5,1,0:T(2,128)S(1)} async-done(((f32[64,1,2,2,2,1,256]{6,2,3,4,5,1,0:T(2,128)}), f32[64,1,2,2,2,1,256]{6,2,3,4,5,1,0:T(2,128)S(1)}, u32[]{:S(2)}, u32[]{:S(2)}) %all-to-all-start.2) | async-done | bytes 524320 | tf_op jit(solution)/shard_map/all_to_all | solution.py:131
  151.9 0.6 convolution_bitcast_fusion.6
  152.6 21.8 %all_to_all.32 = f32[64,1,2,1,256]{4,2,3,1,0:T(2,128)S(1)} all-to-all(f32[64,1,2,1,256]{4,2,3,1,0:T(2,128)S(1)} %copy.44), channel_id=1, replica_groups=mesh['ctx'=64,'tp'=16] {'ctx'}, dimensions={0} | all-to-all | bytes 262144 | tf_op jit(solution)/shard_map/all_to_all | solution.py:131
  174.6 0.7 copy-done.14
  175.3 0.7 convert_multiply_fusion
  176.0 20.4 %all_to_all.33 = f32[64,1,2,1,256]{4,2,3,1,0:T(2,128)S(1)} all-to-all(f32[64,1,2,1,256]{4,2,3,1,0:T(2,128)S(1)} %bitcast.180), channel_id=1, replica_groups=mesh['ctx'=64,'tp'=16] {'ctx'}, dimensions={0} | all-to-all | bytes 262144 | tf_op jit(solution)/shard_map/all_to_all | solution.py:131
  196.5 0.6 convolution_bitcast_fusion.4
  197.4 0.3 copy.47
  197.8 0.3 copy.48
  198.1 0.5 pad_maximum_fusion.1
  198.6 35.6 %all_to_all.34 = f32[64,1,2,2,2,1,256]{6,3,4,2,5,1,0:T(2,128)S(1)} all-to-all(f32[64,1,2,2,2,1,256]{6,3,4,2,5,1,0:T(2,128)S(1)} %pad_maximum_fusion.1), channel_id=1, replica_groups=mesh['ctx'=64,'tp'=16] {'ctx'}, dimensions={0} | all-to-all | bytes 1048576 | tf_op jit(solution)/shard_map/all_to_all | solution.py:131
  234.2 0.8 convolution_bitcast_fusion.3
  235.2 0.7 copy-done.8
  236.0 1.0 convolution_bitcast_fusion
  237.3 0.8 copy.51
  238.1 58.6 %all_to_all.35 = f32[64,1,2,2,2,2,256]{6,5,2,3,4,1,0:T(2,128)S(1)} all-to-all(f32[64,1,2,2,2,2,256]{6,5,2,3,4,1,0:T(2,128)S(1)} %copy.51), channel_id=1, replica_groups=mesh['ctx'=64,'tp'=16] {'ctx'}, dimensions={0} | all-to-all | bytes 2097152 | tf_op jit(solution)/shard_map/all_to_all | solution.py:131
  296.7 1.3 convolution_bitcast_fusion.5
  298.2 27.2 %all_to_all.36 = f32[64,1,2,2,256]{4,3,2,1,0:T(2,128)S(1)} all-to-all(f32[64,1,2,2,256]{4,3,2,1,0:T(2,128)S(1)} %copy.53), channel_id=1, replica_groups=mesh['ctx'=64,'tp'=16] {'ctx'}, dimensions={0} | all-to-all | bytes 524288 | tf_op jit(solution)/shard_map/all_to_all | solution.py:131
  325.4 0.2 slice_multiply_fusion.2
  325.8 3.1 collective-permute-start.1
  328.9 0.7 copy.114
  329.6 1.1 collective-permute-done.1
  330.7 0.3 multiply_reduce_fusion.2
  331.0 409.5 %psum.7 = f32[3,3,256]{2,0,1:T(4,128)S(1)} all-reduce(f32[3,3,256]{2,0,1:T(4,128)S(1)} %pad_maximum_fusion.8), channel_id=1, replica_groups=mesh['ctx'=64,'tp'=16] {'ctx'}, use_global_device_ids=true, to_apply=%region_3.4 | all-reduce | flops 2304 | bytes 18432 | tf_op jit(solution)/shard_map/psum | solution.py:187
  740.5 0.6 copy.55
  741.1 0.7 slice_bitcast_fusion.1
  (63 shorter events, 2.8 us)
Async XLA Ops:
  0.6 6.2 copy-start.15
  0.6 6.2 copy-start.13
  1.4 16.1 %collective-permute-start = (bf16[3,2,256]{2,1,0:T(2,128)(2,1)S(1)}, bf16[3,2,256]{2,1,0:T(2,128)(2,1)S(1)}, u32[]{:S(2)}, u32[]{:S(2)}) collective-permute-start(bf16[3,2,256]{2,1,0:T(2,128)(2,1)S(1)} %pad_maximum_fusion.9), channel_id=1, source_target_pairs={{0,16},{16,32},{32,48},{48,64},{64,80},{80,96},{96,112},{112,128},... | collective-permute-start | bytes 9224 | tf_op jit(solution)/shard_map/ppermute | solution.py:16
  6.9 10.6 %copy-start.4 = (bf16[128,256]{1,0:T(8,128)(2,1)S(1)}, bf16[128,256]{1,0:T(8,128)(2,1)}, u32[]{:S(2)}) copy-start(bf16[128,256]{1,0:T(8,128)(2,1)} %param.8) | copy-start | bytes 196612
  6.9 10.6 %copy-start.5 = (bf16[128,256]{1,0:T(8,128)(2,1)S(1)}, bf16[128,256]{1,0:T(8,128)(2,1)}, u32[]{:S(2)}) copy-start(bf16[128,256]{1,0:T(8,128)(2,1)} %param.7) | copy-start | bytes 196612
  6.9 10.6 %copy-start.6 = (bf16[128,256]{1,0:T(8,128)(2,1)S(1)}, bf16[128,256]{1,0:T(8,128)(2,1)}, u32[]{:S(2)}) copy-start(bf16[128,256]{1,0:T(8,128)(2,1)} %param.6) | copy-start | bytes 196612
  19.0 28.3 %all-to-all-start = ((f32[64,1,2,2,256]{4,3,2,1,0:T(2,128)}), f32[64,1,2,2,256]{4,3,2,1,0:T(2,128)S(1)}, u32[]{:S(2)}, u32[]{:S(2)}) async-start(f32[64,1,2,2,256]{4,3,2,1,0:T(2,128)} %copy.36), calls=%async_computation | async-start | bytes 524288 | tf_op jit(solution)/shard_map/all_to_all | solution.py:131
  52.2 58.2 %all-to-all-start.1 = ((f32[64,1,2,2,2,2,256]{6,3,4,5,2,1,0:T(2,128)}), f32[64,1,2,2,2,2,256]{6,3,4,5,2,1,0:T(2,128)S(1)}, u32[]{:S(2)}, u32[]{:S(2)}) async-start(f32[64,1,2,2,2,2,256]{6,3,4,5,2,1,0:T(2,128)} %pad_maximum_fusion), calls=%async_computation.1 | async-start | bytes 2097152 | tf_op jit(solution)/shard_map/all_to_all | solution.py:131
  59.6 50.8 %copy-start = (f32[1,64,2,128,1]{3,1,0,2,4:T(8,128)}, f32[1,64,2,128,1]{3,1,0,2,4:T(8,128)S(1)}, u32[]{:S(2)}) copy-start(f32[1,64,2,128,1]{3,1,0,2,4:T(8,128)S(1)} %get-tuple-element.57) | copy-start | bytes 196612
  59.6 50.8 %copy-start.2 = (f32[1,64,2,128,1]{3,1,0,2,4:T(8,128)}, f32[1,64,2,128,1]{3,1,0,2,4:T(8,128)S(1)}, u32[]{:S(2)}) copy-start(f32[1,64,2,128,1]{3,1,0,2,4:T(8,128)S(1)} %get-tuple-element.58) | copy-start | bytes 196612
  60.0 52.2 %copy-start.7 = (f32[1,128,64,2,1]{1,2,0,4,3:T(8,128)}, f32[1,128,64,2,1]{1,2,0,4,3:T(8,128)S(1)}, u32[]{:S(2)}) copy-start(f32[1,128,64,2,1]{1,2,0,4,3:T(8,128)S(1)} %get-tuple-element.53) | copy-start | bytes 196612
  60.0 52.2 %copy-start.9 = (f32[1,128,64,2,1]{1,2,0,4,3:T(8,128)}, f32[1,128,64,2,1]{1,2,0,4,3:T(8,128)S(1)}, u32[]{:S(2)}) copy-start(f32[1,128,64,2,1]{1,2,0,4,3:T(8,128)S(1)} %get-tuple-element.54) | copy-start | bytes 196612
  60.0 52.2 %copy-start.11 = (f32[1,128,64,2,1]{1,2,0,4,3:T(8,128)}, f32[1,128,64,2,1]{1,2,0,4,3:T(8,128)S(1)}, u32[]{:S(2)}) copy-start(f32[1,128,64,2,1]{1,2,0,4,3:T(8,128)S(1)} %get-tuple-element.55) | copy-start | bytes 196612
  114.2 37.7 %all-to-all-start.2 = ((f32[64,1,2,2,2,1,256]{6,2,3,4,5,1,0:T(2,128)}), f32[64,1,2,2,2,1,256]{6,2,3,4,5,1,0:T(2,128)S(1)}, u32[]{:S(2)}, u32[]{:S(2)}) async-start(f32[64,1,2,2,2,1,256]{6,2,3,4,5,1,0:T(2,128)} %copy.42), calls=%async_computation.2 | async-start | bytes 1048576 | tf_op jit(solution)/shard_map/all_to_all | solution.py:131
  174.5 0.8 copy-start.14
  198.6 35.6 %copy-start.1 = (f32[1,64,2,128,1]{3,1,0,2,4:T(8,128)S(1)}, f32[1,64,2,128,1]{3,1,0,2,4:T(8,128)}, u32[]{:S(2)}) copy-start(f32[1,64,2,128,1]{3,1,0,2,4:T(8,128)} %copy-done) | copy-start | bytes 196612
  198.6 35.6 %copy-start.3 = (f32[1,64,2,128,1]{3,1,0,2,4:T(8,128)S(1)}, f32[1,64,2,128,1]{3,1,0,2,4:T(8,128)}, u32[]{:S(2)}) copy-start(f32[1,64,2,128,1]{3,1,0,2,4:T(8,128)} %copy-done.2) | copy-start | bytes 196612
  235.1 0.8 copy-start.8
  235.1 0.9 copy-start.10
  235.1 0.9 copy-start.12
  325.8 4.9 collective-permute-start.1
where the time goes:
time: 752 us; the launch traced here: 742 us
  blocking collectives  573 us (76%)
  waiting for transfers between devices  110 us (15%)
  starting transfers between devices  32.6 us (4%)
  local copies, waits for them, and re-layouts  9.72 us (1%)
  matrix products  7.63 us (1%)
    psum x1, blocking collectives, local(): taps_grad = lax.psum(partial_taps, 'ctx') * grad_scale  409 us
    all_to_all x5, blocking collectives, regroup(): lax.all_to_all(blocks, 'ctx', split_axis=0, concat_axis=1, tiled=True)[0]  164 us
    all_to_all x3, waiting for transfers between devices, regroup(): lax.all_to_all(blocks, 'ctx', split_axis=0, concat_axis=1, tiled=True)[0]  98.8 us
    all_to_all x3, starting transfers between devices, regroup(): lax.all_to_all(blocks, 'ctx', split_axis=0, concat_axis=1, tiled=True)[0]  24.1 us
  transfers between devices with their start and end apart: 5, of which 5 were waited for; matrix products, arithmetic and copies ran while one was open for 0% of the time, Pallas kernels for 0%

commit v1 on v0

v1 whole, which is shorter than its diff:
```python
import math

import jax
import jax.numpy as jnp
import ml_dtypes
import numpy as np
from jax import lax
from jax.experimental import pallas as pl
from jax.experimental.pallas import tpu as pltpu
from jax.sharding import PartitionSpec as P

F32 = jnp.float32
BF16 = jnp.bfloat16


def split_np(table):
    high = table.astype(np.float32).astype(ml_dtypes.bfloat16)
    low = (table - high.astype(np.float64)).astype(np.float32).astype(ml_dtypes.bfloat16)
    return high, low


def transform_tables(blocks, width):
    length = blocks * width
    k1 = np.arange(blocks)[:, None] + 0.25
    s = np.arange(blocks)[None, :]
    p = np.arange(width)[None, :]
    angle = 2.0 * np.pi * k1 * s / blocks
    high, low = split_np(np.concatenate([np.cos(angle), -np.sin(angle)], axis=0))
    first = np.concatenate([high, low, high], axis=1)
    twist_angle = 2.0 * np.pi * k1 * p / length
    twist = np.stack([np.cos(twist_angle), -np.sin(twist_angle)]).astype(np.float32)
    p_col = np.arange(width)[:, None]
    k2 = np.arange(width)[None, :]
    angle2 = 2.0 * np.pi * (p_col * k2 % width) / width
    cosine, sine = np.cos(angle2), np.sin(angle2)
    second = np.stack(split_np(np.block([[cosine, -sine], [sine, cosine]])))
    second_back = np.stack(split_np(np.block([[cosine, sine], [-sine, cosine]])))
    high, low = split_np(np.concatenate([np.cos(angle).T, -np.sin(angle).T], axis=1) / length)
    first_back = np.concatenate([high, low, high], axis=1)
    return first, twist, second, second_back, first_back


def halves(x):
    high = x.astype(BF16)
    low = (x - high.astype(F32)).astype(BF16)
    return high, low


def dot(a, b):
    return jnp.dot(a, b, preferred_element_type=F32)


def later(x, offset, lane, row):
    turned = pltpu.roll(x, offset, 1)
    above = jnp.where(row == 0, 0.0, pltpu.roll(turned, 1, 0))
    return jnp.where(lane < offset, above, turned)


def sooner(x, offset, lane, row):
    rows, width = x.shape
    turned = pltpu.roll(x, width - offset, 1)
    below = jnp.where(row == rows - 1, 0.0, pltpu.roll(turned, rows - 1, 0))
    return jnp.where(lane >= width - offset, below, turned)


def layer(load, taps, first, twist, second, second_back, first_back, store, store_sums, channels):
    width = 128
    rows = twist.shape[1]
    lane = lax.broadcasted_iota(jnp.int32, (rows, width), 1)
    row = lax.broadcasted_iota(jnp.int32, (rows, width), 0)
    shifted = {}
    filtered = {}
    for c in range(channels):
        for i in range(3):
            x = load(i, c)
            shifted[i, c] = [x, later(x, 1, lane, row), later(x, 2, lane, row)]
            filtered[i, c] = sum(taps(i, j, c) * shifted[i, c][j] for j in range(3))
    grads = [load(3, c) for c in range(channels)]
    signals = []
    for c in range(channels):
        signals += [filtered[1, c] * filtered[2, c], grads[c] * filtered[0, c]]
    high, low = halves(jnp.concatenate(signals, axis=1))
    spread = dot(first, jnp.concatenate([high, high, low], axis=0))
    filt = jnp.concatenate([load(4, c) for c in range(channels)], axis=1).astype(BF16)
    spread_filt = dot(first[:, : 2 * rows], jnp.concatenate([filt, filt], axis=0))
    turned = []
    for j in range(3 * channels):
        source, at = (spread, j) if j < 2 * channels else (spread_filt, j - 2 * channels)
        re = source[:rows, at * width : (at + 1) * width]
        im = source[rows:, at * width : (at + 1) * width]
        turned.append(jnp.concatenate([re * twist[0] - im * twist[1], re * twist[1] + im * twist[0]], axis=1))
    high, low = halves(jnp.concatenate(turned, axis=0))
    spectra = dot(high, second[0]) + dot(low, second[0]) + dot(high, second[1])

    def spectrum(j):
        block = spectra[j * rows : (j + 1) * rows]
        return block[:, :width], block[:, width:]

    products = []
    for c in range(channels):
        mr, mi = spectrum(2 * c)
        gr, gi = spectrum(2 * c + 1)
        hr, hi = spectrum(2 * channels + c)
        products.append(jnp.concatenate([mr * hr - mi * hi, mr * hi + mi * hr], axis=1))
        products.append(jnp.concatenate([gr * hr + gi * hi, gi * hr - gr * hi], axis=1))
        products.append(jnp.concatenate([gr * mr + gi * mi, gi * mr - gr * mi], axis=1))
    high, low = halves(jnp.concatenate(products, axis=0))
    back = dot(high, second_back[0]) + dot(low, second_back[0]) + dot(high, second_back[1])
    columns = []
    for j in range(3 * channels):
        re = back[j * rows : (j + 1) * rows, :width]
        im = back[j * rows : (j + 1) * rows, width:]
        columns.append(jnp.concatenate([re * twist[0] + im * twist[1], im * twist[0] - re * twist[1]], axis=0))
    high, low = halves(jnp.concatenate(columns, axis=1))
    result = dot(first_back, jnp.concatenate([high, high, low], axis=0))
    scale = 1.0 / math.sqrt(rows * width)
    sums = []
    for c in range(channels):
        convolved, mixed_grad, filter_grad = (
            result[:, (3 * c + j) * width : (3 * c + j + 1) * width] for j in range(3)
        )
        store(0, c, filtered[0, c] * convolved)
        inner = [grads[c] * convolved, mixed_grad * filtered[2, c], mixed_grad * filtered[1, c]]
        for i in range(3):
            g = inner[i]
            grad = taps(i, 0, c) * g + taps(i, 1, c) * sooner(g, 1, lane, row) + taps(i, 2, c) * sooner(g, 2, lane, row)
            store(1 + i, c, grad)
            for j in range(3):
                sums.append(((i, j, c), jnp.sum(g * shifted[i, c][j], axis=0, keepdims=True) * scale))
        store(4, c, filter_grad * scale)
    store_sums(sums)


def layer_kernel(channels, x_ref, taps_ref, first_ref, twist_ref, second_ref, back_ref, first_back_ref, out_ref, grad_ref, sums_ref):
    def load(a, c):
        return x_ref[a * channels + c].astype(F32)

    def taps(i, j, c):
        return taps_ref[(i * 3 + j) * channels + c]

    def store(a, c, value):
        if a < 4:
            out_ref[a * channels + c] = value.astype(BF16)
        else:
            grad_ref[c] = value

    def store_sums(sums):
        for (i, j, c), value in sums:
            at = (i * 3 + j) * channels + c
            sums_ref[at : at + 1, :] = value

    layer(load, taps, first_ref[...], twist_ref[...], second_ref[...], back_ref[...], first_back_ref[...], store, store_sums, channels)


def local(query_in, key_in, value_in, long_filter, short_taps, out_grad):
    rows, width = query_in.shape
    parts = lax.axis_size("ctx")
    me = lax.axis_index("ctx")
    channels = width // parts
    tables = [jnp.asarray(t) for t in transform_tables(parts, rows)]
    inputs = jnp.stack([query_in, key_in, value_in, out_grad, long_filter])
    outgoing = inputs.reshape(5, rows, parts, channels).transpose(2, 0, 3, 1)
    arrived = lax.all_to_all(outgoing, "ctx", split_axis=0, concat_axis=0, tiled=True)
    signals = arrived.transpose(1, 2, 0, 3).reshape(5 * channels, parts, rows)
    my_taps = lax.dynamic_slice_in_dim(short_taps, me * channels, channels, 2).astype(F32).reshape(-1)
    vmem = pl.BlockSpec(memory_space=pltpu.VMEM)
    out, grad, sums = pl.pallas_call(
        lambda *refs: layer_kernel(channels, *refs),
        out_shape=(
            jax.ShapeDtypeStruct((4 * channels, parts, rows), BF16),
            jax.ShapeDtypeStruct((channels, parts, rows), F32),
            jax.ShapeDtypeStruct((9 * channels, rows), F32),
        ),
        in_specs=[vmem, pl.BlockSpec(memory_space=pltpu.SMEM)] + [vmem] * 5,
        out_specs=(vmem, vmem, vmem),
        name="layer",
    )(signals, my_taps, *tables)
    sums = jnp.sum(sums, axis=1)
    sums = jnp.broadcast_to(jnp.pad(sums, (0, rows - sums.shape[0]))[None, None, :], (1, parts, rows))
    wide = jnp.concatenate([grad, sums], axis=0)
    high = lax.reduce_precision(wide, 8, 7)
    low = wide - high
    returning = jnp.concatenate([out, high.astype(BF16), low.astype(BF16)], axis=0).transpose(1, 0, 2)
    returned = lax.all_to_all(returning, "ctx", split_axis=0, concat_axis=0, tiled=True)
    fields = returned[:, : 4 * channels].reshape(parts, 4, channels, rows)
    fields = fields.transpose(1, 3, 0, 2).reshape(4, rows, width)
    high = returned[:, 4 * channels : 5 * channels + 1].astype(F32)
    low = returned[:, 5 * channels + 1 : 6 * channels + 2].astype(F32)
    wide = high + low
    filter_grad = wide[:, :channels].transpose(2, 0, 1).reshape(rows, width)
    taps_grad = wide[:, channels, : 9 * channels].reshape(parts, 3, 3, channels)
    taps_grad = taps_grad.transpose(1, 2, 0, 3).reshape(3, 3, width)
    return fields[0], fields[1], fields[2], fields[3], filter_grad, taps_grad


def solution(mesh):
    placed = P("ctx", "tp")
    taps_placed = P(None, None, "tp")
    return jax.shard_map(
        local,
        mesh=mesh,
        in_specs=(placed, placed, placed, placed, taps_placed, placed),
        out_specs=(placed, placed, placed, placed, placed, taps_placed),
        check_vma=False,
    )
```

time: 752 us -> 97.3 us (0.13); the launches traced: 742 us -> 96.8 us
  blocking collectives: 573 us -> 36.5 us
  waiting for transfers between devices: 110 us -> 20.5 us
  starting transfers between devices: 32.6 us -> 20.2 us
  matrix products: 7.63 us -> 0 us
    psum x1 -> x0, blocking collectives: 409 us -> none  [local(): taps_grad = lax.psum(partial_taps, 'ctx') * grad_scale]
    all_to_all x5 -> x1, blocking collectives: 164 us -> 36.5 us  [local(): lax.all_to_all(returning, 'ctx', split_axis=0, concat_axis=0, tiled=True)]
    all_to_all x3 -> x1, waiting for transfers between devices: 98.8 us -> 20.5 us  [local(): lax.all_to_all(outgoing, 'ctx', split_axis=0, concat_axis=0, tiled=True)]
    ppermute x2 -> x0, waiting for transfers between devices: 11.6 us -> none  [passed_along(): return lax.ppermute(block, axis, route)]
    ppermute x2 -> x0, starting transfers between devices: 8.51 us -> none  [passed_along(): return lax.ppermute(block, axis, route)]
    dot_general x8 -> x0, matrix products: 7.63 us -> none  [the longest x2 2.44 us: spread_forward(): jnp.einsum('pqsrfc,sprkd->qkdfc', arrived, second_table, precision=HIGHES...]
    all_to_all x3 -> x1, starting transfers between devices: 24.1 us -> 20.2 us  [local(): lax.all_to_all(outgoing, 'ctx', split_axis=0, concat_axis=0, tiled=True)]
  transfers between devices with their start and end apart: 5 -> 1, of which waited for: 5 -> 1; matrix products, arithmetic and copies ran while one was open for 0% -> 1% of each run, Pallas kernels for 0% -> 0%
where the time goes in v1:
time: 97.3 us; the launch traced here: 96.8 us
  blocking collectives  36.5 us (38%)
  waiting for transfers between devices  20.5 us (21%)
  starting transfers between devices  20.2 us (21%)
  local copies, waits for them, and re-layouts  12.7 us (13%)
  Pallas kernels  4.03 us (4%)
  other arithmetic  2 us (2%)
    all_to_all x1, blocking collectives, local(): lax.all_to_all(returning, 'ctx', split_axis=0, concat_axis=0, tiled=True)  36.5 us
    all_to_all x1, waiting for transfers between devices, local(): lax.all_to_all(outgoing, 'ctx', split_axis=0, concat_axis=0, tiled=True)  20.5 us
    all_to_all x1, starting transfers between devices, local(): lax.all_to_all(outgoing, 'ctx', split_axis=0, concat_axis=0, tiled=True)  20.2 us
    unnamed x28, local copies, waits for them, and re-layouts  8.79 us
    pallas_call x1, Pallas kernels, local(): pl.pallas_call(lambda *refs: layer_kernel(channels, *refs), out_shape=(ja...  4.03 us
  transfers between devices with their start and end apart: 1, of which 1 were waited for; matrix products, arithmetic and copies ran while one was open for 1% of the time, Pallas kernels for 0%

profile of v1, /device:TPU:1, one launch (start us, length us, event | category | flops | bytes accessed | tf_op | source)
XLA Modules:
  0.0 96.8 jit_solution(13614301818558734158)
XLA Ops:
  0.6 0.0 copy-start.2
  0.6 1.0 %copy.42 = bf16[128,256]{0,1:T(8,128)(2,1)S(1)} copy(bf16[128,256]{1,0:T(8,128)(2,1)} %param.11) | data formatting | bytes 131072 | tf_op args[0]
  1.6 0.0 copy-done.2
  1.6 0.0 copy-start.3
  1.6 0.1 copy.43
  1.8 0.7 copy-done.3
  2.5 0.0 copy-start.4
  2.5 0.1 copy.44
  2.6 0.7 copy-done.4
  3.3 0.0 copy-start.5
  3.3 0.1 copy.46
  3.4 0.7 copy-done.5
  4.2 0.1 copy.45
  4.5 0.8 copy.47
  5.3 20.2 %all-to-all-start = ((bf16[64,5,4,128]{3,2,1,0:T(4,128)(2,1)}), bf16[64,5,4,128]{3,2,1,0:T(4,128)(2,1)S(1)}, u32[]{:S(2)}, u32[]{:S(2)}) async-start(bf16[64,5,4,128]{3,2,1,0:T(4,128)(2,1)} %copy.47), calls=%async_computation | async-start | bytes 655360 | tf_op jit(solution)/shard_map/all_to_all | solution.py:163
  25.6 0.0 copy-start.6
  25.6 0.7 copy-done.6
  26.2 0.1 dynamic-slice_convert_fusion
  26.3 0.6 reshape.59.refs_1_
  26.9 20.5 %all-to-all-done = bf16[64,5,4,128]{3,2,1,0:T(4,128)(2,1)S(1)} async-done(((bf16[64,5,4,128]{3,2,1,0:T(4,128)(2,1)}), bf16[64,5,4,128]{3,2,1,0:T(4,128)(2,1)S(1)}, u32[]{:S(2)}, u32[]{:S(2)}) %all-to-all-start) | async-done | bytes 327712 | tf_op jit(solution)/shard_map/all_to_all | solution.py:163
  47.4 0.8 copy.48
  48.2 4.0 %layer.1 = (bf16[16,64,128]{2,1,0:T(8,128)(2,1)}, f32[4,64,128]{2,1,0:T(8,128)}, f32[36,128]{1,0:T(8,128)}) custom-call(bf16[20,64,128]{2,1,0:T(8,128)(2,1)} %bitcast.26, f32[36]{0:T(128)} %reshape.59.refs_1_, bf16[128,192]{1,0:T(8,128)(2,1)} %constant.25.clone.refs_2_, f32[2,64,128]{2,1,0:T(8,128)} %constant.26.clone.refs_3_, ...), custom_call_target="tpu_custom_call" | custom-call | tf_op jit(solution)/shard_map/layer/pallas_call | solution.py:167
  52.2 0.0 copy-start.1
  52.2 0.9 reduce_sum.9
  53.1 0.9 reduce-precision_convert_fusion
  54.1 0.0 copy-done.1
  54.1 0.1 maximum_bitcast_fusion
  54.1 0.3 copy.49
  54.4 36.5 %all_to_all.10 = bf16[64,26,128]{2,1,0:T(8,128)(2,1)S(1)} all-to-all(bf16[64,26,128]{2,1,0:T(8,128)(2,1)S(1)} %copy.49), channel_id=1, replica_groups=mesh['ctx'=64,'tp'=16] {'ctx'}, dimensions={0} | all-to-all | bytes 851968 | tf_op jit(solution)/shard_map/all_to_all | solution.py:184
  90.9 0.1 convert_add_fusion
  91.0 0.0 copy-start
  91.0 0.7 copy-done
  91.7 0.1 copy.59
  91.8 0.1 fusion.1
  91.9 0.7 copy.56
  92.6 0.0 slice-start
  92.6 0.7 copy.55
  93.4 0.1 copy.51
  93.5 0.1 slice-done
  93.5 0.8 copy.57
  94.3 0.7 copy.54
  95.0 0.7 copy.53
  95.8 0.2 copy.52
  95.9 0.8 reshape.57
  (10 shorter events, 0.3 us)
Async XLA Ops:
  0.6 1.0 %copy-start.2 = (bf16[128,256]{1,0:T(8,128)(2,1)S(1)}, bf16[128,256]{1,0:T(8,128)(2,1)}, u32[]{:S(2)}) copy-start(bf16[128,256]{1,0:T(8,128)(2,1)} %param.12) | copy-start | bytes 196612
  1.6 0.8 copy-start.3
  2.5 0.8 copy-start.4
  3.3 0.8 copy-start.5
  5.3 42.1 %all-to-all-start = ((bf16[64,5,4,128]{3,2,1,0:T(4,128)(2,1)}), bf16[64,5,4,128]{3,2,1,0:T(4,128)(2,1)S(1)}, u32[]{:S(2)}, u32[]{:S(2)}) async-start(bf16[64,5,4,128]{3,2,1,0:T(4,128)(2,1)} %copy.47), calls=%async_computation | async-start | bytes 655360 | tf_op jit(solution)/shard_map/all_to_all | solution.py:163
  25.6 0.7 copy-start.6
  52.2 1.8 %copy-start.1 = (bf16[16,64,128]{2,1,0:T(8,128)(2,1)S(1)}, bf16[16,64,128]{2,1,0:T(8,128)(2,1)}, u32[]{:S(2)}) copy-start(bf16[16,64,128]{2,1,0:T(8,128)(2,1)} %get-tuple-element.9) | copy-start | bytes 786436
  91.0 0.7 copy-start
  92.6 0.9 slice-start

commit v2 on v1

--- a/solution.py
+++ b/solution.py
@@ -131,66 +131,205 @@
     store_sums(sums)
 
 
-def layer_kernel(channels, x_ref, taps_ref, first_ref, twist_ref, second_ref, back_ref, first_back_ref, out_ref, grad_ref, sums_ref):
+MESH = pl.DeviceIdType.MESH
+
+
+def partner(me, step, parts):
+    cores, across = 2, 8 if parts == 64 else parts // 4
+    far = parts // (cores * across)
+    core, z, x = me % cores, (me // cores) % across, me // (cores * across)
+    group = cores * far
+    turn, rest = step // group, group - 1 - step % group
+    shift = across // 2 + (1 - 2 * (turn % 2)) * ((turn + 1) // 2)
+    z_to = (z + shift + across) % across
+    return ((x + rest // cores) % far) * (cores * across) + z_to * cores + (core + rest % cores) % cores
+
+
+def exchange_kernel(parts, channels, q_hbm, k_hbm, v_hbm, g_hbm, h_hbm, taps_ref, first_hbm, twist_hbm, second_hbm, back_hbm, first_back_hbm,
+                    got_ref, got_wide_ref, got_sums_ref,
+                    raw, first_ref, twist_ref, second_ref, back_ref, first_back_ref, tap_rows, wide, wide_h, sum_rows,
+                    send_a, send_h, recv_a, recv_h, send_out, send_wide, send_sums, in_sems, send_sems, recv_sems):
+    me = lax.axis_index("ctx")
+    fields = 4 * channels
+    barrier = pltpu.get_barrier_semaphore()
+
+    def greet(step, carry):
+        pl.semaphore_signal(barrier, inc=1, device_id={"ctx": partner(me, step, parts)}, device_id_type=MESH)
+        return carry
+
+    lax.fori_loop(0, parts - 1, greet, 0)
+    loads = [pltpu.make_async_copy(ref, raw.at[a], in_sems.at[a]) for a, ref in enumerate((q_hbm, k_hbm, v_hbm, g_hbm, h_hbm))]
+    pairs = ((first_hbm, first_ref), (twist_hbm, twist_ref), (second_hbm, second_ref), (back_hbm, back_ref), (first_back_hbm, first_back_ref))
+    tables = [pltpu.make_async_copy(ref, held, in_sems.at[5 + n]) for n, (ref, held) in enumerate(pairs)]
+    for copy in loads + tables:
+        copy.start()
+
+    for a in (4, 0, 1, 2, 3):
+        loads[a].wait()
+        columns = raw[a].astype(F32).T
+        for c in range(channels):
+            block = columns[c * parts : (c + 1) * parts]
+            if a < 4:
+                wide[pl.ds(a * channels + c, parts, stride=fields), :] = block
+            else:
+                wide_h[pl.ds(c, parts, stride=channels), :] = block
+        if a == 4:
+            for d in range(parts):
+                send_h[d] = wide_h[d * channels : (d + 1) * channels, :].astype(BF16)
+    send_a[...] = wide[...].astype(BF16)
+    lane = lax.broadcasted_iota(jnp.int32, (3, taps_ref.shape[2]), 1)
+    for i in range(3):
+        taps_i = taps_ref[i].astype(F32)
+        for c in range(channels):
+            mine = jnp.sum(jnp.where(lane == me + c * parts, taps_i, 0.0), axis=1, keepdims=True)
+            tap_rows[c, 3 * i : 3 * i + 3, :] = jnp.broadcast_to(mine, (3, tap_rows.shape[2]))
+
+    pl.semaphore_wait(barrier, parts - 1)
+
+    def block(ref, d, count):
+        return ref.at[pl.ds(pl.multiple_of(d * count, count), count)]
+
+    def send(step, carry):
+        d = partner(me, step, parts)
+        pltpu.make_async_remote_copy(send_h.at[d], recv_h.at[me], send_sems.at[0], recv_sems.at[0], device_id={"ctx": d}, device_id_type=MESH).start()
+        pltpu.make_async_remote_copy(block(send_a, d, fields), block(recv_a, me, fields), send_sems.at[1], recv_sems.at[1], device_id={"ctx": d}, device_id_type=MESH).start()
+        return carry
+
+    lax.fori_loop(0, parts - 1, send, 0)
+    pltpu.make_async_copy(send_h.at[me], recv_h.at[me], recv_sems.at[0]).start()
+    pltpu.make_async_copy(block(send_a, me, fields), block(recv_a, me, fields), recv_sems.at[1]).start()
+    for copy in tables:
+        copy.wait()
+    pltpu.make_async_copy(recv_h, recv_h, recv_sems.at[0]).wait()
+    pltpu.make_async_copy(recv_a, recv_a, recv_sems.at[1]).wait()
+
+    for d in range(parts):
+        wide_h[d * channels : (d + 1) * channels, :] = recv_h[d].astype(F32)
+    wide[...] = recv_a[...].astype(F32)
+
     def load(a, c):
-        return x_ref[a * channels + c].astype(F32)
+        if a < 4:
+            return wide[pl.ds(a * channels + c, parts, stride=fields), :]
+        return wide_h[pl.ds(c, parts, stride=channels), :]
 
     def taps(i, j, c):
-        return taps_ref[(i * 3 + j) * channels + c]
+        return tap_rows[c, 3 * i + j : 3 * i + j + 1, :]
 
     def store(a, c, value):
         if a < 4:
-            out_ref[a * channels + c] = value.astype(BF16)
+            wide[pl.ds(a * channels + c, parts, stride=fields), :] = value
         else:
-            grad_ref[c] = value
+            wide_h[pl.ds(c, parts, stride=channels), :] = value
 
     def store_sums(sums):
+        sum_rows[...] = jnp.zeros_like(sum_rows)
         for (i, j, c), value in sums:
             at = (i * 3 + j) * channels + c
-            sums_ref[at : at + 1, :] = value
-
-    layer(load, taps, first_ref[...], twist_ref[...], second_ref[...], back_ref[...], first_back_ref[...], store, store_sums, channels)
+            sum_rows[at : at + 1, :] = value
+
+    layer(load, taps, first_ref[...], twist_ref, second_ref, back_ref, first_back_ref[...], store, store_sums, channels)
+    high, low = halves(sum_rows[...])
+    ones = jnp.ones((8, high.shape[1]), BF16)
+    along = (((1,), (1,)), ((), ()))
+    totals = lax.dot_general(ones, high, along, preferred_element_type=F32) + lax.dot_general(ones, low, along, preferred_element_type=F32)
+    send_sums[...] = totals[0:1, :]
+    send_out[...] = wide[...].astype(BF16)
+    for d in range(parts):
+        send_wide[d] = wide_h[d * channels : (d + 1) * channels, :]
+
+    def send_back(step, carry):
+        d = partner(me, step, parts)
+        pltpu.make_async_remote_copy(block(send_out, d, fields), block(got_ref, me, fields), send_sems.at[2], recv_sems.at[2], device_id={"ctx": d}, device_id_type=MESH).start()
+        pltpu.make_async_remote_copy(send_wide.at[d], got_wide_ref.at[me], send_sems.at[3], recv_sems.at[3], device_id={"ctx": d}, device_id_type=MESH).start()
+        pltpu.make_async_remote_copy(send_sums, got_sums_ref.at[me], send_sems.at[4], recv_sems.at[4], device_id={"ctx": d}, device_id_type=MESH).start()
+        return carry
+
+    lax.fori_loop(0, parts - 1, send_back, 0)
+    pltpu.make_async_copy(block(send_out, me, fields), block(got_ref, me, fields), recv_sems.at[2]).start()
+    pltpu.make_async_copy(send_wide.at[me], got_wide_ref.at[me], recv_sems.at[3]).start()
+    pltpu.make_async_copy(send_sums, got_sums_ref.at[me], recv_sems.at[4]).start()
+    others = parts - 1
+    pltpu.make_async_copy(recv_h.at[pl.ds(0, others)], recv_h.at[pl.ds(0, others)], send_sems.at[0]).wait()
+    for n, ref in ((1, recv_a), (2, got_ref)):
+        sent = ref.at[pl.ds(0, others * fields)]
+        pltpu.make_async_copy(sent, sent, send_sems.at[n]).wait()
+    for n, ref in ((3, got_wide_ref), (4, got_sums_ref)):
+        sent = ref.at[pl.ds(0, others)]
+        pltpu.make_async_copy(sent, sent, send_sems.at[n]).wait()
+    for n, ref in ((2, got_ref), (3, got_wide_ref), (4, got_sums_ref)):
+        pltpu.make_async_copy(ref, ref, recv_sems.at[n]).wait()
+
+
+def finish_kernel(parts, channels, got_ref, got_wide_ref, got_sums_ref, out_ref, q_ref, k_ref, v_ref, h_ref, taps_ref, wide, wide_h, sums, turned):
+    fields = 4 * channels
+    wide[...] = got_ref[...].astype(F32)
+    for a, ref in enumerate((out_ref, q_ref, k_ref, v_ref)):
+        blocks = [wide[pl.ds(a * channels + c, parts, stride=fields), :] for c in range(channels)]
+        ref[...] = jnp.concatenate(blocks, axis=0).T.astype(BF16)
+    sums[...] = jnp.zeros_like(sums)
+    for d in range(parts):
+        wide_h[d * channels : (d + 1) * channels, :] = got_wide_ref[d]
+        sums[d : d + 1, :] = got_sums_ref[d]
+    blocks = [wide_h[pl.ds(c, parts, stride=channels), :] for c in range(channels)]
+    h_ref[...] = jnp.concatenate(blocks, axis=0).T
+    turned[...] = sums[...].T
+    rows = jnp.concatenate([turned[pl.ds(c, 16, stride=channels), :][:, :parts] for c in range(channels)], axis=1)
+    for i in range(3):
+        taps_ref[i] = rows[3 * i : 3 * i + 3]
 
 
 def local(query_in, key_in, value_in, long_filter, short_taps, out_grad):
     rows, width = query_in.shape
     parts = lax.axis_size("ctx")
-    me = lax.axis_index("ctx")
     channels = width // parts
+    fields = 4 * channels
     tables = [jnp.asarray(t) for t in transform_tables(parts, rows)]
-    inputs = jnp.stack([query_in, key_in, value_in, out_grad, long_filter])
-    outgoing = inputs.reshape(5, rows, parts, channels).transpose(2, 0, 3, 1)
-    arrived = lax.all_to_all(outgoing, "ctx", split_axis=0, concat_axis=0, tiled=True)
-    signals = arrived.transpose(1, 2, 0, 3).reshape(5 * channels, parts, rows)
-    my_taps = lax.dynamic_slice_in_dim(short_taps, me * channels, channels, 2).astype(F32).reshape(-1)
     vmem = pl.BlockSpec(memory_space=pltpu.VMEM)
-    out, grad, sums = pl.pallas_call(
-        lambda *refs: layer_kernel(channels, *refs),
+    hbm = pl.BlockSpec(memory_space=pl.ANY)
+    got, got_wide, got_sums = pl.pallas_call(
+        lambda *refs: exchange_kernel(parts, channels, *refs),
         out_shape=(
-            jax.ShapeDtypeStruct((4 * channels, parts, rows), BF16),
-            jax.ShapeDtypeStruct((channels, parts, rows), F32),
-            jax.ShapeDtypeStruct((9 * channels, rows), F32),
+            jax.ShapeDtypeStruct((parts * fields, rows), BF16),
+            jax.ShapeDtypeStruct((parts, channels, rows), F32),
+            jax.ShapeDtypeStruct((parts, 1, rows), F32),
         ),
-        in_specs=[vmem, pl.BlockSpec(memory_space=pltpu.SMEM)] + [vmem] * 5,
+        in_specs=[hbm] * 5 + [vmem] + [hbm] * 5,
         out_specs=(vmem, vmem, vmem),
-        name="layer",
-    )(signals, my_taps, *tables)
-    sums = jnp.sum(sums, axis=1)
-    sums = jnp.broadcast_to(jnp.pad(sums, (0, rows - sums.shape[0]))[None, None, :], (1, parts, rows))
-    wide = jnp.concatenate([grad, sums], axis=0)
-    high = lax.reduce_precision(wide, 8, 7)
-    low = wide - high
-    returning = jnp.concatenate([out, high.astype(BF16), low.astype(BF16)], axis=0).transpose(1, 0, 2)
-    returned = lax.all_to_all(returning, "ctx", split_axis=0, concat_axis=0, tiled=True)
-    fields = returned[:, : 4 * channels].reshape(parts, 4, channels, rows)
-    fields = fields.transpose(1, 3, 0, 2).reshape(4, rows, width)
-    high = returned[:, 4 * channels : 5 * channels + 1].astype(F32)
-    low = returned[:, 5 * channels + 1 : 6 * channels + 2].astype(F32)
-    wide = high + low
-    filter_grad = wide[:, :channels].transpose(2, 0, 1).reshape(rows, width)
-    taps_grad = wide[:, channels, : 9 * channels].reshape(parts, 3, 3, channels)
-    taps_grad = taps_grad.transpose(1, 2, 0, 3).reshape(3, 3, width)
-    return fields[0], fields[1], fields[2], fields[3], filter_grad, taps_grad
+        scratch_shapes=[pltpu.VMEM((5, rows, width), BF16)]
+        + [pltpu.VMEM(t.shape, t.dtype) for t in tables]
+        + [
+            pltpu.VMEM((channels, 16, rows), F32),
+            pltpu.VMEM((parts * fields, rows), F32),
+            pltpu.VMEM((parts * channels, rows), F32),
+            pltpu.VMEM((rows, rows), F32),
+            pltpu.VMEM((parts * fields, rows), BF16),
+            pltpu.VMEM((parts, channels, rows), BF16),
+            pltpu.VMEM((parts * fields, rows), BF16),
+            pltpu.VMEM((parts, channels, rows), BF16),
+            pltpu.VMEM((parts * fields, rows), BF16),
+            pltpu.VMEM((parts, channels, rows), F32),
+            pltpu.VMEM((1, rows), F32),
+            pltpu.SemaphoreType.DMA((10,)),
+            pltpu.SemaphoreType.DMA((5,)),
+            pltpu.SemaphoreType.DMA((5,)),
+        ],
+        compiler_params=pltpu.CompilerParams(collective_id=0, has_side_effects=True),
+        name="exchange_and_layer",
+    )(query_in, key_in, value_in, out_grad, long_filter, short_taps, *tables)
+    field = jax.ShapeDtypeStruct((rows, width), BF16)
+    return pl.pallas_call(
+        lambda *refs: finish_kernel(parts, channels, *refs),
+        out_shape=(field, field, field, field, jax.ShapeDtypeStruct((rows, width), F32), jax.ShapeDtypeStruct(short_taps.shape, F32)),
+        in_specs=[vmem] * 3,
+        out_specs=(vmem,) * 6,
+        scratch_shapes=[
+            pltpu.VMEM((parts * fields, rows), F32),
+            pltpu.VMEM((parts * channels, rows), F32),
+            pltpu.VMEM((rows, rows), F32),
+            pltpu.VMEM((rows, rows), F32),
+        ],
+        name="finish",
+    )(got, got_wide, got_sums)
 
 
 def solution(mesh):

time: 97.3 us -> 58.4 us (0.60)
  Pallas kernels: 4.03 us -> 57.6 us
  blocking collectives: 36.5 us -> 0 us
  waiting for transfers between devices: 20.5 us -> 0 us
  starting transfers between devices: 20.2 us -> 0 us
  local copies, waits for them, and re-layouts: 12.7 us -> 0 us
  other arithmetic: 2 us -> 0 us
    pallas_call x1 -> x2, Pallas kernels: 4.03 us -> 57.6 us  [the longest x1 55.5 us: local(): pl.pallas_call(lambda *refs: exchange_kernel(parts, channels, *refs), out...]
    all_to_all x1 -> x0, blocking collectives: 36.5 us -> none  [local(): lax.all_to_all(returning, 'ctx', split_axis=0, concat_axis=0, tiled=True)]
    all_to_all x1 -> x0, waiting for transfers between devices: 20.5 us -> none  [local(): lax.all_to_all(outgoing, 'ctx', split_axis=0, concat_axis=0, tiled=True)]
    all_to_all x1 -> x0, starting transfers between devices: 20.2 us -> none  [local(): lax.all_to_all(outgoing, 'ctx', split_axis=0, concat_axis=0, tiled=True)]
    unnamed x28 -> x0, local copies, waits for them, and re-layouts: 8.79 us -> none
    transpose x4 -> x0, local copies, waits for them, and re-layouts: 2.08 us -> none  [the longest x1 0.84 us: local(): outgoing = inputs.reshape(5, rows, parts, channels).transpose(2, 0, 3, 1)]
    reshape x3 -> x0, local copies, waits for them, and re-layouts: 1.5 us -> none  [the longest x1 0.81 us: local(): taps_grad = taps_grad.transpose(1, 2, 0, 3).reshape(3, 3, width)]
  transfers between devices with their start and end apart: 1 -> 0, of which waited for: 1 -> 0; matrix products, arithmetic and copies ran while one was open for 1% -> 0% of each run, Pallas kernels for 0% -> 0%
where the time goes in v2:
time: 58.4 us; the launch traced here: 58.2 us
  Pallas kernels  57.6 us (99%)
  between operations  0.64 us (1%)
    pallas_call x1, Pallas kernels, local(): pl.pallas_call(lambda *refs: exchange_kernel(parts, channels, *refs), out...  55.5 us
    pallas_call x1, Pallas kernels, local(): pl.pallas_call(lambda *refs: finish_kernel(parts, channels, *refs), out_s...  2.05 us

profile of v2, /device:TPU:1, one launch (start us, length us, event | category | flops | bytes accessed | tf_op | source)
XLA Modules:
  0.0 58.2 jit_solution(13979106849048857201)
XLA Ops:
  0.6 55.5 %exchange_and_layer.1 = (bf16[1024,128]{1,0:T(8,128)(2,1)}, f32[64,4,128]{2,1,0:T(4,128)}, f32[64,1,128]{2,1,0:T(1,128)}) custom-call(bf16[128,256]{1,0:T(8,128)(2,1)} %refs_0_.1, bf16[128,256]{1,0:T(8,128)(2,1)} %refs_1_.1, bf16[128,256]{1,0:T(8,128)(2,1)} %refs_2_.1, bf16[128,256]{1,0:T(8,128)(2,1)} %refs_3_.1, bf16[128,256]{1,0:T(8,128)(2,1)} %refs_4_.1, ...), custom_call_target="tpu_custom_call" | custom-call | tf_op jit(solution)/shard_map/exchange_and_layer/pallas_call | solution.py:289
  56.2 2.0 %finish.1 = (bf16[128,256]{1,0:T(8,128)(2,1)}, bf16[128,256]{1,0:T(8,128)(2,1)}, bf16[128,256]{1,0:T(8,128)(2,1)}, bf16[128,256]{1,0:T(8,128)(2,1)}, f32[128,256]{1,0:T(8,128)}, /*index=5*/f32[3,3,256]{2,1,0:T(4,128)}) custom-call(bf16[1024,128]{1,0:T(8,128)(2,1)} %get-tuple-element.9.refs_0_, f32[64,4,128]{2,1,0:T(4,128)} %get-tuple-element.10.refs_1_, ...), custom_call_target="tpu_custom_call" | custom-call | tf_op jit(solution)/shard_map/finish/pallas_call | solution.py:320

commit v3 on v2

--- a/solution.py
+++ b/solution.py
@@ -132,32 +132,45 @@
 
 
 MESH = pl.DeviceIdType.MESH
-
-
-def partner(me, step, parts):
-    cores, across = 2, 8 if parts == 64 else parts // 4
-    far = parts // (cores * across)
-    core, z, x = me % cores, (me // cores) % across, me // (cores * across)
-    group = cores * far
-    turn, rest = step // group, group - 1 - step % group
-    shift = across // 2 + (1 - 2 * (turn % 2)) * ((turn + 1) // 2)
-    z_to = (z + shift + across) % across
-    return ((x + rest // cores) % far) * (cores * across) + z_to * cores + (core + rest % cores) % cores
-
-
-def exchange_kernel(parts, channels, q_hbm, k_hbm, v_hbm, g_hbm, h_hbm, taps_ref, first_hbm, twist_hbm, second_hbm, back_hbm, first_back_hbm,
+CORES = 2
+
+
+def exchange_kernel(parts, channels, across, q_hbm, k_hbm, v_hbm, g_hbm, h_hbm, taps_ref, first_hbm, twist_hbm, second_hbm, back_hbm, first_back_hbm,
                     got_ref, got_wide_ref, got_sums_ref,
                     raw, first_ref, twist_ref, second_ref, back_ref, first_back_ref, tap_rows, wide, wide_h, sum_rows,
-                    send_a, send_h, recv_a, recv_h, send_out, send_wide, send_sums, in_sems, send_sems, recv_sems):
+                    send_a, send_h, recv_a, recv_h, send_out, send_wide, send_sums, line_sums, in_sems, send_sems, recv_sems):
     me = lax.axis_index("ctx")
-    fields = 4 * channels
+    batch = channels // 2
+    fields = 4 * batch
+    others = parts - 1
+    far = parts // (CORES * across)
+    core, z, x = me % CORES, (me // CORES) % across, me // (CORES * across)
+    plane = [((x + j) % far) * (CORES * across) + (core + k) % CORES for j in range(far) for k in range(CORES)]
+    plane_index = x * CORES + core
+
+    def each_peer(visit):
+        def turn(step, carry):
+            shift = across // 2 + (1 - 2 * (step % 2)) * ((step + 1) // 2)
+            row = ((z + shift) % across) * CORES
+            for base in reversed(plane):
+                visit(base + row)
+            return carry
+
+        lax.fori_loop(0, across - 1, turn, 0)
+        for base in reversed(plane[1:]):
+            visit(base + z * CORES)
+
+    def push(source, target, n, d):
+        pltpu.make_async_remote_copy(source, target, send_sems.at[n], recv_sems.at[n], device_id={"ctx": d}, device_id_type=MESH).start()
+
+    def keep(source, target, n):
+        pltpu.make_async_copy(source, target, recv_sems.at[n]).start()
+
+    def wait_bytes(ref, sem):
+        pltpu.make_async_copy(ref, ref, sem).wait()
+
     barrier = pltpu.get_barrier_semaphore()
-
-    def greet(step, carry):
-        pl.semaphore_signal(barrier, inc=1, device_id={"ctx": partner(me, step, parts)}, device_id_type=MESH)
-        return carry
-
-    lax.fori_loop(0, parts - 1, greet, 0)
+    each_peer(lambda d: pl.semaphore_signal(barrier, inc=1, device_id={"ctx": d}, device_id_type=MESH))
     loads = [pltpu.make_async_copy(ref, raw.at[a], in_sems.at[a]) for a, ref in enumerate((q_hbm, k_hbm, v_hbm, g_hbm, h_hbm))]
     pairs = ((first_hbm, first_ref), (twist_hbm, twist_ref), (second_hbm, second_ref), (back_hbm, back_ref), (first_back_hbm, first_back_ref))
     tables = [pltpu.make_async_copy(ref, held, in_sems.at[5 + n]) for n, (ref, held) in enumerate(pairs)]
@@ -170,13 +183,14 @@
         for c in range(channels):
             block = columns[c * parts : (c + 1) * parts]
             if a < 4:
-                wide[pl.ds(a * channels + c, parts, stride=fields), :] = block
+                wide[c // batch, pl.ds(a * batch + c % batch, parts, stride=fields), :] = block
             else:
                 wide_h[pl.ds(c, parts, stride=channels), :] = block
         if a == 4:
             for d in range(parts):
                 send_h[d] = wide_h[d * channels : (d + 1) * channels, :].astype(BF16)
-    send_a[...] = wide[...].astype(BF16)
+    for b in range(2):
+        send_a[b] = wide[b].reshape(parts, fields, wide.shape[2]).astype(BF16)
     lane = lax.broadcasted_iota(jnp.int32, (3, taps_ref.shape[2]), 1)
     for i in range(3):
         taps_i = taps_ref[i].astype(F32)
@@ -184,92 +198,97 @@
             mine = jnp.sum(jnp.where(lane == me + c * parts, taps_i, 0.0), axis=1, keepdims=True)
             tap_rows[c, 3 * i : 3 * i + 3, :] = jnp.broadcast_to(mine, (3, tap_rows.shape[2]))
 
-    pl.semaphore_wait(barrier, parts - 1)
-
-    def block(ref, d, count):
-        return ref.at[pl.ds(pl.multiple_of(d * count, count), count)]
-
-    def send(step, carry):
-        d = partner(me, step, parts)
-        pltpu.make_async_remote_copy(send_h.at[d], recv_h.at[me], send_sems.at[0], recv_sems.at[0], device_id={"ctx": d}, device_id_type=MESH).start()
-        pltpu.make_async_remote_copy(block(send_a, d, fields), block(recv_a, me, fields), send_sems.at[1], recv_sems.at[1], device_id={"ctx": d}, device_id_type=MESH).start()
-        return carry
-
-    lax.fori_loop(0, parts - 1, send, 0)
-    pltpu.make_async_copy(send_h.at[me], recv_h.at[me], recv_sems.at[0]).start()
-    pltpu.make_async_copy(block(send_a, me, fields), block(recv_a, me, fields), recv_sems.at[1]).start()
+    pl.semaphore_wait(barrier, others)
+
+    def send_first(d):
+        push(send_h.at[d], recv_h.at[me], 0, d)
+        push(send_a.at[0, d], recv_a.at[0, me], 1, d)
+
+    each_peer(send_first)
+    each_peer(lambda d: push(send_a.at[1, d], recv_a.at[1, me], 2, d))
+    keep(send_h.at[me], recv_h.at[me], 0)
+    for b in range(2):
+        keep(send_a.at[b, me], recv_a.at[b, me], 1 + b)
     for copy in tables:
         copy.wait()
-    pltpu.make_async_copy(recv_h, recv_h, recv_sems.at[0]).wait()
-    pltpu.make_async_copy(recv_a, recv_a, recv_sems.at[1]).wait()
-
-    for d in range(parts):
-        wide_h[d * channels : (d + 1) * channels, :] = recv_h[d].astype(F32)
-    wide[...] = recv_a[...].astype(F32)
-
-    def load(a, c):
-        if a < 4:
-            return wide[pl.ds(a * channels + c, parts, stride=fields), :]
-        return wide_h[pl.ds(c, parts, stride=channels), :]
-
-    def taps(i, j, c):
-        return tap_rows[c, 3 * i + j : 3 * i + j + 1, :]
-
-    def store(a, c, value):
-        if a < 4:
-            wide[pl.ds(a * channels + c, parts, stride=fields), :] = value
-        else:
-            wide_h[pl.ds(c, parts, stride=channels), :] = value
-
-    def store_sums(sums):
-        sum_rows[...] = jnp.zeros_like(sum_rows)
-        for (i, j, c), value in sums:
-            at = (i * 3 + j) * channels + c
-            sum_rows[at : at + 1, :] = value
-
-    layer(load, taps, first_ref[...], twist_ref, second_ref, back_ref, first_back_ref[...], store, store_sums, channels)
+    sum_rows[...] = jnp.zeros_like(sum_rows)
+
+    def run(b):
+        if b == 0:
+            wait_bytes(recv_h, recv_sems.at[0])
+            for d in range(parts):
+                wide_h[d * channels : (d + 1) * channels, :] = recv_h[d].astype(F32)
+        wait_bytes(recv_a.at[b], recv_sems.at[1 + b])
+        wide[b] = recv_a[b].astype(F32).reshape(parts * fields, wide.shape[2])
+
+        def load(a, c):
+            if a < 4:
+                return wide[b, pl.ds(a * batch + c, parts, stride=fields), :]
+            return wide_h[pl.ds(b * batch + c, parts, stride=channels), :]
+
+        def taps(i, j, c):
+            return tap_rows[b * batch + c, 3 * i + j : 3 * i + j + 1, :]
+
+        def store(a, c, value):
+            if a < 4:
+                wide[b, pl.ds(a * batch + c, parts, stride=fields), :] = value
+            else:
+                wide_h[pl.ds(b * batch + c, parts, stride=channels), :] = value
+
+        def store_sums(sums):
+            for (i, j, c), value in sums:
+                at = (i * 3 + j) * channels + b * batch + c
+                sum_rows[at : at + 1, :] = value
+
+        layer(load, taps, first_ref[...], twist_ref, second_ref, back_ref, first_back_ref[...], store, store_sums, batch)
+        send_out[b] = wide[b].reshape(parts, fields, wide.shape[2]).astype(BF16)
+
+    run(0)
+    each_peer(lambda d: push(send_out.at[0, d], got_ref.at[0, me], 3, d))
+    keep(send_out.at[0, me], got_ref.at[0, me], 3)
+    run(1)
     high, low = halves(sum_rows[...])
     ones = jnp.ones((8, high.shape[1]), BF16)
     along = (((1,), (1,)), ((), ()))
     totals = lax.dot_general(ones, high, along, preferred_element_type=F32) + lax.dot_general(ones, low, along, preferred_element_type=F32)
     send_sums[...] = totals[0:1, :]
-    send_out[...] = wide[...].astype(BF16)
     for d in range(parts):
         send_wide[d] = wide_h[d * channels : (d + 1) * channels, :]
-
-    def send_back(step, carry):
-        d = partner(me, step, parts)
-        pltpu.make_async_remote_copy(block(send_out, d, fields), block(got_ref, me, fields), send_sems.at[2], recv_sems.at[2], device_id={"ctx": d}, device_id_type=MESH).start()
-        pltpu.make_async_remote_copy(send_wide.at[d], got_wide_ref.at[me], send_sems.at[3], recv_sems.at[3], device_id={"ctx": d}, device_id_type=MESH).start()
-        pltpu.make_async_remote_copy(send_sums, got_sums_ref.at[me], send_sems.at[4], recv_sems.at[4], device_id={"ctx": d}, device_id_type=MESH).start()
-        return carry
-
-    lax.fori_loop(0, parts - 1, send_back, 0)
-    pltpu.make_async_copy(block(send_out, me, fields), block(got_ref, me, fields), recv_sems.at[2]).start()
-    pltpu.make_async_copy(send_wide.at[me], got_wide_ref.at[me], recv_sems.at[3]).start()
-    pltpu.make_async_copy(send_sums, got_sums_ref.at[me], recv_sems.at[4]).start()
-    others = parts - 1
-    pltpu.make_async_copy(recv_h.at[pl.ds(0, others)], recv_h.at[pl.ds(0, others)], send_sems.at[0]).wait()
-    for n, ref in ((1, recv_a), (2, got_ref)):
-        sent = ref.at[pl.ds(0, others * fields)]
-        pltpu.make_async_copy(sent, sent, send_sems.at[n]).wait()
-    for n, ref in ((3, got_wide_ref), (4, got_sums_ref)):
-        sent = ref.at[pl.ds(0, others)]
-        pltpu.make_async_copy(sent, sent, send_sems.at[n]).wait()
-    for n, ref in ((2, got_ref), (3, got_wide_ref), (4, got_sums_ref)):
-        pltpu.make_async_copy(ref, ref, recv_sems.at[n]).wait()
-
-
-def finish_kernel(parts, channels, got_ref, got_wide_ref, got_sums_ref, out_ref, q_ref, k_ref, v_ref, h_ref, taps_ref, wide, wide_h, sums, turned):
-    fields = 4 * channels
-    wide[...] = got_ref[...].astype(F32)
+    for k in range(1, across):
+        push(send_sums, line_sums.at[z], 6, plane[0] + ((z + k) % across) * CORES)
+    keep(send_sums, line_sums.at[z], 6)
+
+    def send_last(d):
+        push(send_out.at[1, d], got_ref.at[1, me], 4, d)
+        push(send_wide.at[d], got_wide_ref.at[me], 5, d)
+
+    each_peer(send_last)
+    keep(send_out.at[1, me], got_ref.at[1, me], 4)
+    keep(send_wide.at[me], got_wide_ref.at[me], 5)
+    wait_bytes(line_sums, recv_sems.at[6])
+    for base in plane[1:]:
+        push(line_sums, got_sums_ref.at[plane_index], 7, base + z * CORES)
+    keep(line_sums, got_sums_ref.at[plane_index], 7)
+    for n, ref in enumerate((recv_h, recv_a.at[0], recv_a.at[1], got_ref.at[0], got_ref.at[1], got_wide_ref, line_sums, got_sums_ref)):
+        sent = ref.at[pl.ds(0, ref.shape[0] - 1)]
+        wait_bytes(sent, send_sems.at[n])
+    for n, ref in ((3, got_ref.at[0]), (4, got_ref.at[1]), (5, got_wide_ref), (7, got_sums_ref)):
+        wait_bytes(ref, recv_sems.at[n])
+
+
+def finish_kernel(parts, channels, across, got_ref, got_wide_ref, got_sums_ref, out_ref, q_ref, k_ref, v_ref, h_ref, taps_ref, wide, wide_h, sums, turned):
+    batch = channels // 2
+    fields = 4 * batch
+    for b in range(2):
+        wide[b] = got_ref[b].astype(F32).reshape(parts * fields, wide.shape[2])
     for a, ref in enumerate((out_ref, q_ref, k_ref, v_ref)):
-        blocks = [wide[pl.ds(a * channels + c, parts, stride=fields), :] for c in range(channels)]
+        blocks = [wide[c // batch, pl.ds(a * batch + c % batch, parts, stride=fields), :] for c in range(channels)]
         ref[...] = jnp.concatenate(blocks, axis=0).T.astype(BF16)
     sums[...] = jnp.zeros_like(sums)
     for d in range(parts):
         wide_h[d * channels : (d + 1) * channels, :] = got_wide_ref[d]
-        sums[d : d + 1, :] = got_sums_ref[d]
+        at = d // (CORES * across) * CORES + d % CORES
+        sums[d : d + 1, :] = got_sums_ref[at, (d // CORES) % across]
     blocks = [wide_h[pl.ds(c, parts, stride=channels), :] for c in range(channels)]
     h_ref[...] = jnp.concatenate(blocks, axis=0).T
     turned[...] = sums[...].T
@@ -281,17 +300,20 @@
 def local(query_in, key_in, value_in, long_filter, short_taps, out_grad):
     rows, width = query_in.shape
     parts = lax.axis_size("ctx")
+    across = 8 if parts == 64 else parts // 4
     channels = width // parts
-    fields = 4 * channels
+    fields = 2 * channels
     tables = [jnp.asarray(t) for t in transform_tables(parts, rows)]
     vmem = pl.BlockSpec(memory_space=pltpu.VMEM)
     hbm = pl.BlockSpec(memory_space=pl.ANY)
-    got, got_wide, got_sums = pl.pallas_call(
-        lambda *refs: exchange_kernel(parts, channels, *refs),
+    planes = parts // across
+    both = (2, parts, fields, rows)
+    got = pl.pallas_call(
+        lambda *refs: exchange_kernel(parts, channels, across, *refs),
         out_shape=(
-            jax.ShapeDtypeStruct((parts * fields, rows), BF16),
+            jax.ShapeDtypeStruct(both, BF16),
             jax.ShapeDtypeStruct((parts, channels, rows), F32),
-            jax.ShapeDtypeStruct((parts, 1, rows), F32),
+            jax.ShapeDtypeStruct((planes, across, 1, rows), F32),
         ),
         in_specs=[hbm] * 5 + [vmem] + [hbm] * 5,
         out_specs=(vmem, vmem, vmem),
@@ -299,37 +321,38 @@
         + [pltpu.VMEM(t.shape, t.dtype) for t in tables]
         + [
             pltpu.VMEM((channels, 16, rows), F32),
-            pltpu.VMEM((parts * fields, rows), F32),
+            pltpu.VMEM((2, parts * fields, rows), F32),
             pltpu.VMEM((parts * channels, rows), F32),
             pltpu.VMEM((rows, rows), F32),
-            pltpu.VMEM((parts * fields, rows), BF16),
+            pltpu.VMEM(both, BF16),
             pltpu.VMEM((parts, channels, rows), BF16),
-            pltpu.VMEM((parts * fields, rows), BF16),
+            pltpu.VMEM(both, BF16),
             pltpu.VMEM((parts, channels, rows), BF16),
-            pltpu.VMEM((parts * fields, rows), BF16),
+            pltpu.VMEM(both, BF16),
             pltpu.VMEM((parts, channels, rows), F32),
             pltpu.VMEM((1, rows), F32),
+            pltpu.VMEM((across, 1, rows), F32),
             pltpu.SemaphoreType.DMA((10,)),
-            pltpu.SemaphoreType.DMA((5,)),
-            pltpu.SemaphoreType.DMA((5,)),
+            pltpu.SemaphoreType.DMA((8,)),
+            pltpu.SemaphoreType.DMA((8,)),
         ],
         compiler_params=pltpu.CompilerParams(collective_id=0, has_side_effects=True),
         name="exchange_and_layer",
     )(query_in, key_in, value_in, out_grad, long_filter, short_taps, *tables)
     field = jax.ShapeDtypeStruct((rows, width), BF16)
     return pl.pallas_call(
-        lambda *refs: finish_kernel(parts, channels, *refs),
+        lambda *refs: finish_kernel(parts, channels, across, *refs),
         out_shape=(field, field, field, field, jax.ShapeDtypeStruct((rows, width), F32), jax.ShapeDtypeStruct(short_taps.shape, F32)),
         in_specs=[vmem] * 3,
         out_specs=(vmem,) * 6,
         scratch_shapes=[
-            pltpu.VMEM((parts * fields, rows), F32),
+            pltpu.VMEM((2, parts * fields, rows), F32),
             pltpu.VMEM((parts * channels, rows), F32),
             pltpu.VMEM((rows, rows), F32),
             pltpu.VMEM((rows, rows), F32),
         ],
         name="finish",
-    )(got, got_wide, got_sums)
+    )(*got)
 
 
 def solution(mesh):

time: 58.4 us -> 57.2 us (0.979)
  Pallas kernels: 57.6 us -> 56.3 us
    pallas_call x2, Pallas kernels: 57.6 us -> 56.3 us  [the longest x1 54.2 us: local(): pl.pallas_call(lambda *refs: exchange_kernel(parts, channels, across, *re...]
where the time goes in v3:
time: 57.2 us; the launch traced here: 56.9 us
  Pallas kernels  56.3 us (98%)
  between operations  0.64 us (1%)
    pallas_call x1, Pallas kernels, local(): pl.pallas_call(lambda *refs: exchange_kernel(parts, channels, across, *re...  54.2 us
    pallas_call x1, Pallas kernels, local(): pl.pallas_call(lambda *refs: finish_kernel(parts, channels, across, *refs...  2.05 us

profile of v3, /device:TPU:1, one launch (start us, length us, event | category | flops | bytes accessed | tf_op | source)
XLA Modules:
  0.0 56.9 jit_solution(16224360312298748746)
XLA Ops:
  0.6 54.2 %exchange_and_layer.1 = (bf16[2,64,8,128]{3,2,1,0:T(8,128)(2,1)}, f32[64,4,128]{2,1,0:T(4,128)}, f32[8,8,1,128]{3,2,1,0:T(1,128)}) custom-call(bf16[128,256]{1,0:T(8,128)(2,1)} %refs_0_.1, bf16[128,256]{1,0:T(8,128)(2,1)} %refs_1_.1, bf16[128,256]{1,0:T(8,128)(2,1)} %refs_2_.1, bf16[128,256]{1,0:T(8,128)(2,1)} %refs_3_.1, bf16[128,256]{1,0:T(8,128)(2,1)} %refs_4_.1, ...), custom_call_target="tpu_custom_call" | custom-call | tf_op jit(solution)/shard_map/exchange_and_layer/pallas_call | solution.py:311
  54.9 2.1 %finish.1 = (bf16[128,256]{1,0:T(8,128)(2,1)}, bf16[128,256]{1,0:T(8,128)(2,1)}, bf16[128,256]{1,0:T(8,128)(2,1)}, bf16[128,256]{1,0:T(8,128)(2,1)}, f32[128,256]{1,0:T(8,128)}, /*index=5*/f32[3,3,256]{2,1,0:T(4,128)}) custom-call(bf16[2,64,8,128]{3,2,1,0:T(8,128)(2,1)} %get-tuple-element.9.refs_0_, f32[64,4,128]{2,1,0:T(4,128)} %get-tuple-element.10.refs_1_, ...), custom_call_target="tpu_custom_call" | custom-call | tf_op jit(solution)/shard_map/finish/pallas_call | solution.py:343

commit v4 on v3

--- a/solution.py
+++ b/solution.py
@@ -135,9 +135,9 @@
 CORES = 2
 
 
-def exchange_kernel(parts, channels, across, q_hbm, k_hbm, v_hbm, g_hbm, h_hbm, taps_ref, first_hbm, twist_hbm, second_hbm, back_hbm, first_back_hbm,
+def exchange_kernel(parts, channels, across, q_hbm, k_hbm, v_hbm, g_hbm, h_hbm, taps_hbm, first_hbm, twist_hbm, second_hbm, back_hbm, first_back_hbm,
                     got_ref, got_wide_ref, got_sums_ref,
-                    raw, first_ref, twist_ref, second_ref, back_ref, first_back_ref, tap_rows, wide, wide_h, sum_rows,
+                    raw, taps_ref, first_ref, twist_ref, second_ref, back_ref, first_back_ref, tap_rows, wide, wide_h, sum_rows,
                     send_a, send_h, recv_a, recv_h, send_out, send_wide, send_sums, line_sums, in_sems, send_sems, recv_sems):
     me = lax.axis_index("ctx")
     batch = channels // 2
@@ -172,7 +172,7 @@
     barrier = pltpu.get_barrier_semaphore()
     each_peer(lambda d: pl.semaphore_signal(barrier, inc=1, device_id={"ctx": d}, device_id_type=MESH))
     loads = [pltpu.make_async_copy(ref, raw.at[a], in_sems.at[a]) for a, ref in enumerate((q_hbm, k_hbm, v_hbm, g_hbm, h_hbm))]
-    pairs = ((first_hbm, first_ref), (twist_hbm, twist_ref), (second_hbm, second_ref), (back_hbm, back_ref), (first_back_hbm, first_back_ref))
+    pairs = ((taps_hbm, taps_ref), (first_hbm, first_ref), (twist_hbm, twist_ref), (second_hbm, second_ref), (back_hbm, back_ref), (first_back_hbm, first_back_ref))
     tables = [pltpu.make_async_copy(ref, held, in_sems.at[5 + n]) for n, (ref, held) in enumerate(pairs)]
     for copy in loads + tables:
         copy.start()
@@ -191,6 +191,7 @@
                 send_h[d] = wide_h[d * channels : (d + 1) * channels, :].astype(BF16)
     for b in range(2):
         send_a[b] = wide[b].reshape(parts, fields, wide.shape[2]).astype(BF16)
+    tables[0].wait()
     lane = lax.broadcasted_iota(jnp.int32, (3, taps_ref.shape[2]), 1)
     for i in range(3):
         taps_i = taps_ref[i].astype(F32)
@@ -209,7 +210,7 @@
     keep(send_h.at[me], recv_h.at[me], 0)
     for b in range(2):
         keep(send_a.at[b, me], recv_a.at[b, me], 1 + b)
-    for copy in tables:
+    for copy in tables[1:]:
         copy.wait()
     sum_rows[...] = jnp.zeros_like(sum_rows)
 
@@ -276,25 +277,36 @@
         wait_bytes(ref, recv_sems.at[n])
 
 
-def finish_kernel(parts, channels, across, got_ref, got_wide_ref, got_sums_ref, out_ref, q_ref, k_ref, v_ref, h_ref, taps_ref, wide, wide_h, sums, turned):
+def finish_kernel(parts, channels, across, got_ref, got_wide_ref, got_sums_ref, out_hbm, q_hbm, k_hbm, v_hbm, h_hbm, taps_hbm,
+                  wide, wide_h, sums, turned, done, done_h, done_taps, sems):
     batch = channels // 2
     fields = 4 * batch
-    for b in range(2):
-        wide[b] = got_ref[b].astype(F32).reshape(parts * fields, wide.shape[2])
-    for a, ref in enumerate((out_ref, q_ref, k_ref, v_ref)):
-        blocks = [wide[c // batch, pl.ds(a * batch + c % batch, parts, stride=fields), :] for c in range(channels)]
-        ref[...] = jnp.concatenate(blocks, axis=0).T.astype(BF16)
-    sums[...] = jnp.zeros_like(sums)
+    copies = []
+
+    def put(source, target):
+        copies.append(pltpu.make_async_copy(source, target, sems.at[len(copies)]))
+        copies[-1].start()
+
     for d in range(parts):
         wide_h[d * channels : (d + 1) * channels, :] = got_wide_ref[d]
         at = d // (CORES * across) * CORES + d % CORES
         sums[d : d + 1, :] = got_sums_ref[at, (d // CORES) % across]
     blocks = [wide_h[pl.ds(c, parts, stride=channels), :] for c in range(channels)]
-    h_ref[...] = jnp.concatenate(blocks, axis=0).T
+    done_h[...] = jnp.concatenate(blocks, axis=0).T
+    put(done_h, h_hbm)
     turned[...] = sums[...].T
-    rows = jnp.concatenate([turned[pl.ds(c, 16, stride=channels), :][:, :parts] for c in range(channels)], axis=1)
+    rows = jnp.concatenate([turned[pl.ds(c, 9, stride=channels), :] for c in range(channels)], axis=1)
     for i in range(3):
-        taps_ref[i] = rows[3 * i : 3 * i + 3]
+        done_taps[i] = rows[3 * i : 3 * i + 3]
+    put(done_taps, taps_hbm)
+    for b in range(2):
+        wide[b] = got_ref[b].astype(F32).reshape(parts * fields, wide.shape[2])
+    for a, ref in enumerate((out_hbm, q_hbm, k_hbm, v_hbm)):
+        blocks = [wide[c // batch, pl.ds(a * batch + c % batch, parts, stride=fields), :] for c in range(channels)]
+        done[a] = jnp.concatenate(blocks, axis=0).T.astype(BF16)
+        put(done.at[a], ref)
+    for copy in copies:
+        copy.wait()
 
 
 def local(query_in, key_in, value_in, long_filter, short_taps, out_grad):
@@ -311,13 +323,13 @@
     got = pl.pallas_call(
         lambda *refs: exchange_kernel(parts, channels, across, *refs),
         out_shape=(
-            jax.ShapeDtypeStruct(both, BF16),
-            jax.ShapeDtypeStruct((parts, channels, rows), F32),
-            jax.ShapeDtypeStruct((planes, across, 1, rows), F32),
+            pltpu.VMEM(both, BF16),
+            pltpu.VMEM((parts, channels, rows), F32),
+            pltpu.VMEM((planes, across, 1, rows), F32),
         ),
-        in_specs=[hbm] * 5 + [vmem] + [hbm] * 5,
+        in_specs=[hbm] * 11,
         out_specs=(vmem, vmem, vmem),
-        scratch_shapes=[pltpu.VMEM((5, rows, width), BF16)]
+        scratch_shapes=[pltpu.VMEM((5, rows, width), BF16), pltpu.VMEM(short_taps.shape, BF16)]
         + [pltpu.VMEM(t.shape, t.dtype) for t in tables]
         + [
             pltpu.VMEM((channels, 16, rows), F32),
@@ -332,24 +344,29 @@
             pltpu.VMEM((parts, channels, rows), F32),
             pltpu.VMEM((1, rows), F32),
             pltpu.VMEM((across, 1, rows), F32),
-            pltpu.SemaphoreType.DMA((10,)),
+            pltpu.SemaphoreType.DMA((11,)),
             pltpu.SemaphoreType.DMA((8,)),
             pltpu.SemaphoreType.DMA((8,)),
         ],
         compiler_params=pltpu.CompilerParams(collective_id=0, has_side_effects=True),
         name="exchange_and_layer",
     )(query_in, key_in, value_in, out_grad, long_filter, short_taps, *tables)
+    got = [pltpu.with_memory_space_constraint(g, pltpu.VMEM) for g in got]
     field = jax.ShapeDtypeStruct((rows, width), BF16)
     return pl.pallas_call(
         lambda *refs: finish_kernel(parts, channels, across, *refs),
         out_shape=(field, field, field, field, jax.ShapeDtypeStruct((rows, width), F32), jax.ShapeDtypeStruct(short_taps.shape, F32)),
         in_specs=[vmem] * 3,
-        out_specs=(vmem,) * 6,
+        out_specs=(hbm,) * 6,
         scratch_shapes=[
             pltpu.VMEM((2, parts * fields, rows), F32),
             pltpu.VMEM((parts * channels, rows), F32),
-            pltpu.VMEM((rows, rows), F32),
-            pltpu.VMEM((rows, rows), F32),
+            pltpu.VMEM((parts, rows), F32),
+            pltpu.VMEM((rows, parts), F32),
+            pltpu.VMEM((4, rows, width), BF16),
+            pltpu.VMEM((rows, width), F32),
+            pltpu.VMEM(short_taps.shape, F32),
+            pltpu.SemaphoreType.DMA((6,)),
         ],
         name="finish",
     )(*got)

time: 57.2 us -> 54.9 us (0.960)
  Pallas kernels: 56.3 us -> 54.1 us
    pallas_call x1, Pallas kernels: 54.2 us -> 53.1 us  [local(): pl.pallas_call(lambda *refs: exchange_kernel(parts, channels, across, *re...]
    pallas_call x1, Pallas kernels: 2.05 us -> 1.01 us  [local(): pl.pallas_call(lambda *refs: finish_kernel(parts, channels, across, *refs...]
where the time goes in v4:
time: 54.9 us; the launch traced here: 54.7 us
  Pallas kernels  54.1 us (99%)
  between operations  0.64 us (1%)
    pallas_call x1, Pallas kernels, local(): pl.pallas_call(lambda *refs: exchange_kernel(parts, channels, across, *re...  53.1 us

profile of v4, /device:TPU:1, one launch (start us, length us, event | category | flops | bytes accessed | tf_op | source)
XLA Modules:
  0.0 54.7 jit_solution(4147246998737741800)
XLA Ops:
  0.6 53.1 %exchange_and_layer.1 = (bf16[2,64,8,128]{3,2,1,0:T(8,128)(2,1)S(1)}, f32[64,4,128]{2,1,0:T(4,128)S(1)}, f32[8,8,1,128]{3,2,1,0:T(1,128)S(1)}) custom-call(bf16[128,256]{1,0:T(8,128)(2,1)} %refs_0_.1, bf16[128,256]{1,0:T(8,128)(2,1)} %refs_1_.1, bf16[128,256]{1,0:T(8,128)(2,1)} %refs_2_.1, bf16[128,256]{1,0:T(8,128)(2,1)} %refs_3_.1, ...), custom_call_target="tpu_custom_call" | custom-call | tf_op jit(solution)/shard_map/exchange_and_layer/pallas_call | solution.py:323
  53.7 1.0 %finish.1 = (bf16[128,256]{1,0:T(8,128)(2,1)}, bf16[128,256]{1,0:T(8,128)(2,1)}, bf16[128,256]{1,0:T(8,128)(2,1)}, bf16[128,256]{1,0:T(8,128)(2,1)}, f32[128,256]{1,0:T(8,128)}, /*index=5*/f32[3,3,256]{2,1,0:T(4,128)}) custom-call(bf16[2,64,8,128]{3,2,1,0:T(8,128)(2,1)S(1)} %get-tuple-element.9.refs_0_, f32[64,4,128]{2,1,0:T(4,128)S(1)} %get-tuple-element.10.refs_1_, ...), custom_call_target="tpu_custom_call" | custom-call | tf_op jit(solution)/shard_map/finish/pallas_call | solution.py:356

commit v5 on v4

--- a/solution.py
+++ b/solution.py
@@ -138,7 +138,7 @@
 def exchange_kernel(parts, channels, across, q_hbm, k_hbm, v_hbm, g_hbm, h_hbm, taps_hbm, first_hbm, twist_hbm, second_hbm, back_hbm, first_back_hbm,
                     got_ref, got_wide_ref, got_sums_ref,
                     raw, taps_ref, first_ref, twist_ref, second_ref, back_ref, first_back_ref, tap_rows, wide, wide_h, sum_rows,
-                    send_a, send_h, recv_a, recv_h, send_out, send_wide, send_sums, line_sums, in_sems, send_sems, recv_sems):
+                    send_a, send_h, recv_a, recv_h, send_out, send_wide, send_sums, line_sums, in_sems, send_sems, recv_sems, entered):
     me = lax.axis_index("ctx")
     batch = channels // 2
     fields = 4 * batch
@@ -169,8 +169,30 @@
     def wait_bytes(ref, sem):
         pltpu.make_async_copy(ref, ref, sem).wait()
 
+    apart = lax.axis_index("tp") == 0
+    last = apart & (me == 0)
+    spots = [j * (CORES * across) + k for j in range(far) for k in range(CORES)]
     barrier = pltpu.get_barrier_semaphore()
-    each_peer(lambda d: pl.semaphore_signal(barrier, inc=1, device_id={"ctx": d}, device_id_type=MESH))
+
+    def tell(sem, d):
+        pl.semaphore_signal(sem, inc=1, device_id={"ctx": d}, device_id_type=MESH)
+
+    def in_rows(d):
+        return jnp.logical_not(apart & (d == 0))
+
+    @pl.when(jnp.logical_not(last))
+    def _():
+        def greet_row(row, carry):
+            for spot in spots:
+                tell(barrier, spot + row * CORES)
+            return carry
+
+        for base in plane[1:]:
+            d = base + z * CORES
+            pl.when(in_rows(d))(lambda d=d: tell(barrier, d))
+        lax.fori_loop(z + 1, across, greet_row, 0)
+        pl.when(apart)(lambda: tell(barrier, 0))
+
     loads = [pltpu.make_async_copy(ref, raw.at[a], in_sems.at[a]) for a, ref in enumerate((q_hbm, k_hbm, v_hbm, g_hbm, h_hbm))]
     pairs = ((taps_hbm, taps_ref), (first_hbm, first_ref), (twist_hbm, twist_ref), (second_hbm, second_ref), (back_hbm, back_ref), (first_back_hbm, first_back_ref))
     tables = [pltpu.make_async_copy(ref, held, in_sems.at[5 + n]) for n, (ref, held) in enumerate(pairs)]
@@ -199,14 +221,50 @@
             mine = jnp.sum(jnp.where(lane == me + c * parts, taps_i, 0.0), axis=1, keepdims=True)
             tap_rows[c, 3 * i : 3 * i + 3, :] = jnp.broadcast_to(mine, (3, tap_rows.shape[2]))
 
-    pl.semaphore_wait(barrier, others)
+    known = jnp.where(apart, len(spots) * (z + 1) - 2, len(spots) * (z + 1) - 1)
+    pl.semaphore_wait(barrier, jnp.where(last, others, known))
+
+    @pl.when(jnp.logical_not(last))
+    def _():
+        def tell_row(row, carry):
+            for spot in spots[1:]:
+                tell(entered.at[z], spot + row * CORES)
+            pl.when(in_rows(row * CORES))(lambda: tell(entered.at[z], row * CORES))
+            return carry
+
+        lax.fori_loop(0, z, tell_row, 0)
+
+    @pl.when(last)
+    def _():
+        each_peer(lambda d: tell(entered.at[across], d))
+
+    def each_in_rows(visit, wait):
+        def to_row(row, carry):
+            if wait:
+                pl.when((row > z) & jnp.logical_not(last))(lambda: pl.semaphore_wait(entered.at[row], len(spots)))
+            for spot in spots:
+                d = spot + row * CORES
+                pl.when((d != me) & in_rows(d))(lambda d=d: visit(d))
+            return carry
+
+        lax.fori_loop(0, across, to_row, 0)
 
     def send_first(d):
         push(send_h.at[d], recv_h.at[me], 0, d)
         push(send_a.at[0, d], recv_a.at[0, me], 1, d)
 
-    each_peer(send_first)
-    each_peer(lambda d: push(send_a.at[1, d], recv_a.at[1, me], 2, d))
+    def send_second(d):
+        push(send_a.at[1, d], recv_a.at[1, me], 2, d)
+
+    each_in_rows(send_first, True)
+    each_in_rows(send_second, False)
+
+    @pl.when(apart & (me != 0))
+    def _():
+        pl.semaphore_wait(entered.at[across], 1)
+        send_first(0)
+        send_second(0)
+
     keep(send_h.at[me], recv_h.at[me], 0)
     for b in range(2):
         keep(send_a.at[b, me], recv_a.at[b, me], 1 + b)
@@ -347,6 +405,7 @@
             pltpu.SemaphoreType.DMA((11,)),
             pltpu.SemaphoreType.DMA((8,)),
             pltpu.SemaphoreType.DMA((8,)),
+            pltpu.SemaphoreType.REGULAR((across + 1,)),
         ],
         compiler_params=pltpu.CompilerParams(collective_id=0, has_side_effects=True),
         name="exchange_and_layer",

time: 54.9 us -> 54.8 us (level)
  no operation moved by 1% of the time
where the time goes in v5:
time: 54.8 us; the launch traced here: 54.2 us
  Pallas kernels  53.6 us (98%)
  between operations  0.64 us (1%)
    pallas_call x1, Pallas kernels, local(): pl.pallas_call(lambda *refs: exchange_kernel(parts, channels, across, *re...  52.6 us

profile of v5, /device:TPU:1, one launch (start us, length us, event | category | flops | bytes accessed | tf_op | source)
XLA Modules:
  0.0 54.2 jit_solution(16022013725443076247)
XLA Ops:
  0.6 52.6 %exchange_and_layer.1 = (bf16[2,64,8,128]{3,2,1,0:T(8,128)(2,1)S(1)}, f32[64,4,128]{2,1,0:T(4,128)S(1)}, f32[8,8,1,128]{3,2,1,0:T(1,128)S(1)}) custom-call(bf16[128,256]{1,0:T(8,128)(2,1)} %refs_0_.1, bf16[128,256]{1,0:T(8,128)(2,1)} %refs_1_.1, bf16[128,256]{1,0:T(8,128)(2,1)} %refs_2_.1, bf16[128,256]{1,0:T(8,128)(2,1)} %refs_3_.1, ...), custom_call_target="tpu_custom_call" | custom-call | tf_op jit(solution)/shard_map/exchange_and_layer/pallas_call | solution.py:381
  53.2 1.0 %finish.1 = (bf16[128,256]{1,0:T(8,128)(2,1)}, bf16[128,256]{1,0:T(8,128)(2,1)}, bf16[128,256]{1,0:T(8,128)(2,1)}, bf16[128,256]{1,0:T(8,128)(2,1)}, f32[128,256]{1,0:T(8,128)}, /*index=5*/f32[3,3,256]{2,1,0:T(4,128)}) custom-call(bf16[2,64,8,128]{3,2,1,0:T(8,128)(2,1)S(1)} %get-tuple-element.9.refs_0_, f32[64,4,128]{2,1,0:T(4,128)S(1)} %get-tuple-element.10.refs_1_, ...), custom_call_target="tpu_custom_call" | custom-call | tf_op jit(solution)/shard_map/finish/pallas_call | solution.py:415

commit v6 on v4

--- a/solution.py
+++ b/solution.py
@@ -137,23 +137,28 @@
 
 def exchange_kernel(parts, channels, across, q_hbm, k_hbm, v_hbm, g_hbm, h_hbm, taps_hbm, first_hbm, twist_hbm, second_hbm, back_hbm, first_back_hbm,
                     got_ref, got_wide_ref, got_sums_ref,
-                    raw, taps_ref, first_ref, twist_ref, second_ref, back_ref, first_back_ref, tap_rows, wide, wide_h, sum_rows,
-                    send_a, send_h, recv_a, recv_h, send_out, send_wide, send_sums, line_sums, in_sems, send_sems, recv_sems):
+                    raw, taps_ref, first_ref, twist_ref, second_ref, back_ref, first_back_ref, tap_rows, wide, wide_h, grad_rows, sum_rows,
+                    send_a, send_h, recv_a, recv_h, send_out, send_wide, send_sums, line_sums, in_sems, send_sems, recv_sems, entered):
     me = lax.axis_index("ctx")
-    batch = channels // 2
-    fields = 4 * batch
+    fields = 4
     others = parts - 1
     far = parts // (CORES * across)
     core, z, x = me % CORES, (me // CORES) % across, me // (CORES * across)
     plane = [((x + j) % far) * (CORES * across) + (core + k) % CORES for j in range(far) for k in range(CORES)]
     plane_index = x * CORES + core
 
-    def each_peer(visit):
+    staged = lax.axis_index("tp") % 2 == 0
+    apart = lax.axis_index("tp") == 0
+    last = apart & (me == 0)
+
+    def each_peer(visit, early_first=False):
         def turn(step, carry):
             shift = across // 2 + (1 - 2 * (step % 2)) * ((step + 1) // 2)
-            row = ((z + shift) % across) * CORES
+            row = (z + shift) % across
+            if early_first:
+                row = jnp.where(staged, jnp.where(step < z, step, step + 1), row)
             for base in reversed(plane):
-                visit(base + row)
+                visit(base + row * CORES)
             return carry
 
         lax.fori_loop(0, across - 1, turn, 0)
@@ -169,13 +174,54 @@
     def wait_bytes(ref, sem):
         pltpu.make_async_copy(ref, ref, sem).wait()
 
+    spots = [j * (CORES * across) + k for j in range(far) for k in range(CORES)]
     barrier = pltpu.get_barrier_semaphore()
-    each_peer(lambda d: pl.semaphore_signal(barrier, inc=1, device_id={"ctx": d}, device_id_type=MESH))
+
+    def tell(sem, d):
+        pl.semaphore_signal(sem, inc=1, device_id={"ctx": d}, device_id_type=MESH)
+
+    def in_rows(d):
+        return jnp.logical_not(apart & (d == 0))
+
+    @pl.when(jnp.logical_not(staged))
+    def _():
+        each_peer(lambda d: tell(barrier, d))
+
+    @pl.when(staged & jnp.logical_not(last))
+    def _():
+        def greet_row(row, carry):
+            for spot in spots:
+                tell(barrier, spot + row * CORES)
+            return carry
+
+        for base in plane[1:]:
+            d = base + z * CORES
+            pl.when(in_rows(d))(lambda d=d: tell(barrier, d))
+        lax.fori_loop(z + 1, across, greet_row, 0)
+        pl.when(apart)(lambda: tell(barrier, 0))
+
     loads = [pltpu.make_async_copy(ref, raw.at[a], in_sems.at[a]) for a, ref in enumerate((q_hbm, k_hbm, v_hbm, g_hbm, h_hbm))]
     pairs = ((taps_hbm, taps_ref), (first_hbm, first_ref), (twist_hbm, twist_ref), (second_hbm, second_ref), (back_hbm, back_ref), (first_back_hbm, first_back_ref))
     tables = [pltpu.make_async_copy(ref, held, in_sems.at[5 + n]) for n, (ref, held) in enumerate(pairs)]
     for copy in loads + tables:
         copy.start()
+
+    known = jnp.where(apart, len(spots) * (z + 1) - 2, len(spots) * (z + 1) - 1)
+    pl.semaphore_wait(barrier, jnp.where(last | jnp.logical_not(staged), others, known))
+
+    @pl.when(staged & jnp.logical_not(last))
+    def _():
+        def tell_row(row, carry):
+            for spot in spots[1:]:
+                tell(entered.at[z], spot + row * CORES)
+            pl.when(in_rows(row * CORES))(lambda: tell(entered.at[z], row * CORES))
+            return carry
+
+        lax.fori_loop(0, z, tell_row, 0)
+
+    @pl.when(last)
+    def _():
+        each_peer(lambda d: tell(entered.at[across], d))
 
     for a in (4, 0, 1, 2, 3):
         loads[a].wait()
@@ -183,14 +229,16 @@
         for c in range(channels):
             block = columns[c * parts : (c + 1) * parts]
             if a < 4:
-                wide[c // batch, pl.ds(a * batch + c % batch, parts, stride=fields), :] = block
+                wide[c, pl.ds(a, parts, stride=fields), :] = block
             else:
-                wide_h[pl.ds(c, parts, stride=channels), :] = block
+                wide_h[c // 2, pl.ds(c % 2, parts, stride=2), :] = block
         if a == 4:
-            for d in range(parts):
-                send_h[d] = wide_h[d * channels : (d + 1) * channels, :].astype(BF16)
-    for b in range(2):
-        send_a[b] = wide[b].reshape(parts, fields, wide.shape[2]).astype(BF16)
+            for b in range(2):
+                for d in range(parts):
+                    send_h[b, d] = wide_h[b, 2 * d : 2 * d + 2, :].astype(BF16)
+    for c in range(channels):
+        for d in range(parts):
+            send_a[c, d] = wide[c, d * fields : (d + 1) * fields, :].astype(BF16)
     tables[0].wait()
     lane = lax.broadcasted_iota(jnp.int32, (3, taps_ref.shape[2]), 1)
     for i in range(3):
@@ -199,88 +247,132 @@
             mine = jnp.sum(jnp.where(lane == me + c * parts, taps_i, 0.0), axis=1, keepdims=True)
             tap_rows[c, 3 * i : 3 * i + 3, :] = jnp.broadcast_to(mine, (3, tap_rows.shape[2]))
 
-    pl.semaphore_wait(barrier, others)
-
-    def send_first(d):
-        push(send_h.at[d], recv_h.at[me], 0, d)
-        push(send_a.at[0, d], recv_a.at[0, me], 1, d)
-
-    each_peer(send_first)
-    each_peer(lambda d: push(send_a.at[1, d], recv_a.at[1, me], 2, d))
-    keep(send_h.at[me], recv_h.at[me], 0)
+    def to_row(visit, row):
+        for spot in spots:
+            d = spot + row * CORES
+            pl.when((d != me) & in_rows(d))(lambda d=d: visit(d))
+
+    def send_chunk(c, d, pair=None):
+        if pair is not None:
+            push(send_h.at[pair, d], recv_h.at[pair, me], 4 + pair, d)
+        push(send_a.at[c, d], recv_a.at[c, me], c, d)
+
+    sends = [lambda d: send_chunk(0, d, 0), lambda d: send_chunk(1, d), lambda d: send_chunk(2, d, 1), lambda d: send_chunk(3, d)]
+
+    def to_rows(visit):
+        def step(row, carry):
+            to_row(visit, row)
+            return carry
+
+        return step
+
+    def next_row(row, carry):
+        to_row(sends[1], row - 1)
+        pl.semaphore_wait(entered.at[row], len(spots))
+        to_row(sends[0], row)
+        return carry
+
+    @pl.when(staged)
+    def _():
+        inside = jnp.where(last, across - 1, z)
+        lax.fori_loop(0, inside + 1, to_rows(sends[0]), 0)
+        lax.fori_loop(0, inside, to_rows(sends[1]), 0)
+        lax.fori_loop(inside + 1, across, next_row, 0)
+        to_row(sends[1], across - 1)
+        lax.fori_loop(0, across, to_rows(sends[2]), 0)
+        lax.fori_loop(0, across, to_rows(sends[3]), 0)
+
+    @pl.when(jnp.logical_not(staged))
+    def _():
+        for visit in sends:
+            each_peer(visit)
+
+    @pl.when(apart & (me != 0))
+    def _():
+        pl.semaphore_wait(entered.at[across], 1)
+        for visit in sends:
+            visit(0)
+
     for b in range(2):
-        keep(send_a.at[b, me], recv_a.at[b, me], 1 + b)
+        keep(send_h.at[b, me], recv_h.at[b, me], 4 + b)
+    for c in range(channels):
+        keep(send_a.at[c, me], recv_a.at[c, me], c)
     for copy in tables[1:]:
         copy.wait()
     sum_rows[...] = jnp.zeros_like(sum_rows)
 
-    def run(b):
-        if b == 0:
-            wait_bytes(recv_h, recv_sems.at[0])
+    def run(c, carry):
+        @pl.when(c % 2 == 0)
+        def _():
+            wait_bytes(recv_h.at[c // 2], recv_sems.at[4 + c // 2])
             for d in range(parts):
-                wide_h[d * channels : (d + 1) * channels, :] = recv_h[d].astype(F32)
-        wait_bytes(recv_a.at[b], recv_sems.at[1 + b])
-        wide[b] = recv_a[b].astype(F32).reshape(parts * fields, wide.shape[2])
-
-        def load(a, c):
+                wide_h[c // 2, 2 * d : 2 * d + 2, :] = recv_h[c // 2, d].astype(F32)
+
+        wait_bytes(recv_a.at[c], recv_sems.at[c])
+        for d in range(parts):
+            wide[c, d * fields : (d + 1) * fields, :] = recv_a[c, d].astype(F32)
+
+        def load(a, _):
             if a < 4:
-                return wide[b, pl.ds(a * batch + c, parts, stride=fields), :]
-            return wide_h[pl.ds(b * batch + c, parts, stride=channels), :]
-
-        def taps(i, j, c):
-            return tap_rows[b * batch + c, 3 * i + j : 3 * i + j + 1, :]
-
-        def store(a, c, value):
+                return wide[c, pl.ds(a, parts, stride=fields), :]
+            return wide_h[c // 2, pl.ds(c % 2, parts, stride=2), :]
+
+        def taps(i, j, _):
+            return tap_rows[c, 3 * i + j : 3 * i + j + 1, :]
+
+        def store(a, _, value):
             if a < 4:
-                wide[b, pl.ds(a * batch + c, parts, stride=fields), :] = value
+                wide[c, pl.ds(a, parts, stride=fields), :] = value
             else:
-                wide_h[pl.ds(b * batch + c, parts, stride=channels), :] = value
+                grad_rows[c] = value
 
         def store_sums(sums):
-            for (i, j, c), value in sums:
-                at = (i * 3 + j) * channels + b * batch + c
-                sum_rows[at : at + 1, :] = value
-
-        layer(load, taps, first_ref[...], twist_ref, second_ref, back_ref, first_back_ref[...], store, store_sums, batch)
-        send_out[b] = wide[b].reshape(parts, fields, wide.shape[2]).astype(BF16)
-
-    run(0)
-    each_peer(lambda d: push(send_out.at[0, d], got_ref.at[0, me], 3, d))
-    keep(send_out.at[0, me], got_ref.at[0, me], 3)
-    run(1)
-    high, low = halves(sum_rows[...])
-    ones = jnp.ones((8, high.shape[1]), BF16)
-    along = (((1,), (1,)), ((), ()))
-    totals = lax.dot_general(ones, high, along, preferred_element_type=F32) + lax.dot_general(ones, low, along, preferred_element_type=F32)
-    send_sums[...] = totals[0:1, :]
-    for d in range(parts):
-        send_wide[d] = wide_h[d * channels : (d + 1) * channels, :]
-    for k in range(1, across):
-        push(send_sums, line_sums.at[z], 6, plane[0] + ((z + k) % across) * CORES)
-    keep(send_sums, line_sums.at[z], 6)
-
-    def send_last(d):
-        push(send_out.at[1, d], got_ref.at[1, me], 4, d)
-        push(send_wide.at[d], got_wide_ref.at[me], 5, d)
-
-    each_peer(send_last)
-    keep(send_out.at[1, me], got_ref.at[1, me], 4)
-    keep(send_wide.at[me], got_wide_ref.at[me], 5)
-    wait_bytes(line_sums, recv_sems.at[6])
+            for (i, j, _), value in sums:
+                sum_rows[c, 3 * i + j : 3 * i + j + 1, :] = value
+
+        layer(load, taps, first_ref[...], twist_ref, second_ref, back_ref, first_back_ref[...], store, store_sums, 1)
+        for d in range(parts):
+            send_out[c, d] = wide[c, d * fields : (d + 1) * fields, :].astype(BF16)
+            send_wide[c, d] = grad_rows[c, d : d + 1, :]
+
+        def send_back(d):
+            push(send_out.at[c, d], got_ref.at[c, me], 6 + c, d)
+            push(send_wide.at[c, d], got_wide_ref.at[c, me], 10 + c, d)
+
+        @pl.when(c == channels - 1)
+        def _():
+            high, low = halves(sum_rows[...].reshape(channels * 16, sum_rows.shape[2]))
+            high = jnp.concatenate([high, jnp.zeros_like(high)], axis=0)
+            low = jnp.concatenate([low, jnp.zeros_like(low)], axis=0)
+            ones = jnp.ones((8, high.shape[1]), BF16)
+            along = (((1,), (1,)), ((), ()))
+            totals = lax.dot_general(ones, high, along, preferred_element_type=F32) + lax.dot_general(ones, low, along, preferred_element_type=F32)
+            send_sums[...] = totals[0:1, :]
+            for k in range(1, across):
+                push(send_sums, line_sums.at[z], 14, plane[0] + ((z + k) % across) * CORES)
+            keep(send_sums, line_sums.at[z], 14)
+
+        each_peer(send_back, True)
+        keep(send_out.at[c, me], got_ref.at[c, me], 6 + c)
+        keep(send_wide.at[c, me], got_wide_ref.at[c, me], 10 + c)
+        return carry
+
+    lax.fori_loop(0, channels, run, 0)
+    wait_bytes(line_sums, recv_sems.at[14])
     for base in plane[1:]:
-        push(line_sums, got_sums_ref.at[plane_index], 7, base + z * CORES)
-    keep(line_sums, got_sums_ref.at[plane_index], 7)
-    for n, ref in enumerate((recv_h, recv_a.at[0], recv_a.at[1], got_ref.at[0], got_ref.at[1], got_wide_ref, line_sums, got_sums_ref)):
-        sent = ref.at[pl.ds(0, ref.shape[0] - 1)]
-        wait_bytes(sent, send_sems.at[n])
-    for n, ref in ((3, got_ref.at[0]), (4, got_ref.at[1]), (5, got_wide_ref), (7, got_sums_ref)):
-        wait_bytes(ref, recv_sems.at[n])
+        push(line_sums, got_sums_ref.at[plane_index], 15, base + z * CORES)
+    keep(line_sums, got_sums_ref.at[plane_index], 15)
+    sent = [recv_a.at[c] for c in range(channels)] + [recv_h.at[b] for b in range(2)]
+    sent += [got_ref.at[c] for c in range(channels)] + [got_wide_ref.at[c] for c in range(channels)] + [line_sums, got_sums_ref]
+    for n, ref in enumerate(sent):
+        wait_bytes(ref.at[pl.ds(0, ref.shape[0] - 1)], send_sems.at[n])
+    for n in (*range(6, 14), 15):
+        wait_bytes(sent[n], recv_sems.at[n])
 
 
 def finish_kernel(parts, channels, across, got_ref, got_wide_ref, got_sums_ref, out_hbm, q_hbm, k_hbm, v_hbm, h_hbm, taps_hbm,
                   wide, wide_h, sums, turned, done, done_h, done_taps, sems):
-    batch = channels // 2
-    fields = 4 * batch
+    fields = 4
     copies = []
 
     def put(source, target):
@@ -288,21 +380,22 @@
         copies[-1].start()
 
     for d in range(parts):
-        wide_h[d * channels : (d + 1) * channels, :] = got_wide_ref[d]
+        for c in range(channels):
+            wide_h[c * parts + d : c * parts + d + 1, :] = got_wide_ref[c, d]
         at = d // (CORES * across) * CORES + d % CORES
         sums[d : d + 1, :] = got_sums_ref[at, (d // CORES) % across]
-    blocks = [wide_h[pl.ds(c, parts, stride=channels), :] for c in range(channels)]
-    done_h[...] = jnp.concatenate(blocks, axis=0).T
+    done_h[...] = wide_h[...].T
     put(done_h, h_hbm)
     turned[...] = sums[...].T
-    rows = jnp.concatenate([turned[pl.ds(c, 9, stride=channels), :] for c in range(channels)], axis=1)
+    rows = jnp.concatenate([turned[16 * c : 16 * c + 9, :] for c in range(channels)], axis=1)
     for i in range(3):
         done_taps[i] = rows[3 * i : 3 * i + 3]
     put(done_taps, taps_hbm)
-    for b in range(2):
-        wide[b] = got_ref[b].astype(F32).reshape(parts * fields, wide.shape[2])
+    for c in range(channels):
+        for d in range(parts):
+            wide[c, d * fields : (d + 1) * fields, :] = got_ref[c, d].astype(F32)
     for a, ref in enumerate((out_hbm, q_hbm, k_hbm, v_hbm)):
-        blocks = [wide[c // batch, pl.ds(a * batch + c % batch, parts, stride=fields), :] for c in range(channels)]
+        blocks = [wide[c, pl.ds(a, parts, stride=fields), :] for c in range(channels)]
         done[a] = jnp.concatenate(blocks, axis=0).T.astype(BF16)
         put(done.at[a], ref)
     for copy in copies:
@@ -314,17 +407,18 @@
     parts = lax.axis_size("ctx")
     across = 8 if parts == 64 else parts // 4
     channels = width // parts
-    fields = 2 * channels
+    fields = 4
     tables = [jnp.asarray(t) for t in transform_tables(parts, rows)]
     vmem = pl.BlockSpec(memory_space=pltpu.VMEM)
     hbm = pl.BlockSpec(memory_space=pl.ANY)
     planes = parts // across
-    both = (2, parts, fields, rows)
+    chunks = (channels, parts, fields, rows)
+    pairs = (2, parts, 2, rows)
     got = pl.pallas_call(
         lambda *refs: exchange_kernel(parts, channels, across, *refs),
         out_shape=(
-            pltpu.VMEM(both, BF16),
-            pltpu.VMEM((parts, channels, rows), F32),
+            pltpu.VMEM(chunks, BF16),
+            pltpu.VMEM((channels, parts, 1, rows), F32),
             pltpu.VMEM((planes, across, 1, rows), F32),
         ),
         in_specs=[hbm] * 11,
@@ -333,20 +427,22 @@
         + [pltpu.VMEM(t.shape, t.dtype) for t in tables]
         + [
             pltpu.VMEM((channels, 16, rows), F32),
-            pltpu.VMEM((2, parts * fields, rows), F32),
-            pltpu.VMEM((parts * channels, rows), F32),
-            pltpu.VMEM((rows, rows), F32),
-            pltpu.VMEM(both, BF16),
-            pltpu.VMEM((parts, channels, rows), BF16),
-            pltpu.VMEM(both, BF16),
-            pltpu.VMEM((parts, channels, rows), BF16),
-            pltpu.VMEM(both, BF16),
-            pltpu.VMEM((parts, channels, rows), F32),
+            pltpu.VMEM((channels, parts * fields, rows), F32),
+            pltpu.VMEM((2, parts * 2, rows), F32),
+            pltpu.VMEM((channels, parts, rows), F32),
+            pltpu.VMEM((channels, 16, rows), F32),
+            pltpu.VMEM(chunks, BF16),
+            pltpu.VMEM(pairs, BF16),
+            pltpu.VMEM(chunks, BF16),
+            pltpu.VMEM(pairs, BF16),
+            pltpu.VMEM(chunks, BF16),
+            pltpu.VMEM((channels, parts, 1, rows), F32),
             pltpu.VMEM((1, rows), F32),
             pltpu.VMEM((across, 1, rows), F32),
             pltpu.SemaphoreType.DMA((11,)),
-            pltpu.SemaphoreType.DMA((8,)),
-            pltpu.SemaphoreType.DMA((8,)),
+            pltpu.SemaphoreType.DMA((16,)),
+            pltpu.SemaphoreType.DMA((16,)),
+            pltpu.SemaphoreType.REGULAR((across + 1,)),
         ],
         compiler_params=pltpu.CompilerParams(collective_id=0, has_side_effects=True),
         name="exchange_and_layer",
@@ -359,7 +455,7 @@
         in_specs=[vmem] * 3,
         out_specs=(hbm,) * 6,
         scratch_shapes=[
-            pltpu.VMEM((2, parts * fields, rows), F32),
+            pltpu.VMEM((channels, parts * fields, rows), F32),
             pltpu.VMEM((parts * channels, rows), F32),
             pltpu.VMEM((parts, rows), F32),
             pltpu.VMEM((rows, parts), F32),

time: 54.9 us -> 53.1 us (0.967)
  Pallas kernels: 54.1 us -> 52.3 us
    pallas_call x1, Pallas kernels: 53.1 us -> 51.3 us  [local(): pl.pallas_call(lambda *refs: exchange_kernel(parts, channels, across, *re...]
where the time goes in v6:
time: 53.1 us; the launch traced here: 53 us
  Pallas kernels  52.3 us (98%)
  between operations  0.64 us (1%)
    pallas_call x1, Pallas kernels, local(): pl.pallas_call(lambda *refs: exchange_kernel(parts, channels, across, *re...  51.3 us

profile of v6, /device:TPU:1, one launch (start us, length us, event | category | flops | bytes accessed | tf_op | source)
XLA Modules:
  0.0 53.0 jit_solution(10342807602360474940)
XLA Ops:
  0.6 51.3 %exchange_and_layer.1 = (bf16[4,64,4,128]{3,2,1,0:T(4,128)(2,1)S(1)}, f32[4,64,1,128]{3,2,1,0:T(1,128)S(1)}, f32[8,8,1,128]{3,2,1,0:T(1,128)S(1)}) custom-call(bf16[128,256]{1,0:T(8,128)(2,1)} %refs_0_.1, bf16[128,256]{1,0:T(8,128)(2,1)} %refs_1_.1, bf16[128,256]{1,0:T(8,128)(2,1)} %refs_2_.1, bf16[128,256]{1,0:T(8,128)(2,1)} %refs_3_.1, ...), custom_call_target="tpu_custom_call" | custom-call | tf_op jit(solution)/shard_map/exchange_and_layer/pallas_call | solution.py:417
  52.0 1.0 %finish.1 = (bf16[128,256]{1,0:T(8,128)(2,1)}, bf16[128,256]{1,0:T(8,128)(2,1)}, bf16[128,256]{1,0:T(8,128)(2,1)}, bf16[128,256]{1,0:T(8,128)(2,1)}, f32[128,256]{1,0:T(8,128)}, /*index=5*/f32[3,3,256]{2,1,0:T(4,128)}) custom-call(bf16[4,64,4,128]{3,2,1,0:T(4,128)(2,1)S(1)} %get-tuple-element.9.refs_0_, f32[4,64,1,128]{3,2,1,0:T(1,128)S(1)} %get-tuple-element.10.refs_1_, ...), custom_call_target="tpu_custom_call" | custom-call | tf_op jit(solution)/shard_map/finish/pallas_call | solution.py:452

commit v7 on v4

--- a/solution.py
+++ b/solution.py
@@ -148,12 +148,16 @@
     plane = [((x + j) % far) * (CORES * across) + (core + k) % CORES for j in range(far) for k in range(CORES)]
     plane_index = x * CORES + core
 
-    def each_peer(visit):
+    skewed = lax.axis_index("tp") % 2 == 0
+
+    def each_peer(visit, early_first=False):
         def turn(step, carry):
             shift = across // 2 + (1 - 2 * (step % 2)) * ((step + 1) // 2)
-            row = ((z + shift) % across) * CORES
+            row = (z + shift) % across
+            if early_first:
+                row = jnp.where(skewed, jnp.where(step < z, step, step + 1), row)
             for base in reversed(plane):
-                visit(base + row)
+                visit(base + row * CORES)
             return carry
 
         lax.fori_loop(0, across - 1, turn, 0)
@@ -243,37 +247,38 @@
 
         layer(load, taps, first_ref[...], twist_ref, second_ref, back_ref, first_back_ref[...], store, store_sums, batch)
         send_out[b] = wide[b].reshape(parts, fields, wide.shape[2]).astype(BF16)
+        for d in range(parts):
+            send_wide[b, d] = wide_h[d * channels + b * batch : d * channels + (b + 1) * batch, :]
+
+    def send_back(b):
+        def visit(d):
+            push(send_out.at[b, d], got_ref.at[b, me], 3 + b, d)
+            push(send_wide.at[b, d], got_wide_ref.at[b, me], 5 + b, d)
+
+        each_peer(visit, True)
+        keep(send_out.at[b, me], got_ref.at[b, me], 3 + b)
+        keep(send_wide.at[b, me], got_wide_ref.at[b, me], 5 + b)
 
     run(0)
-    each_peer(lambda d: push(send_out.at[0, d], got_ref.at[0, me], 3, d))
-    keep(send_out.at[0, me], got_ref.at[0, me], 3)
+    send_back(0)
     run(1)
     high, low = halves(sum_rows[...])
     ones = jnp.ones((8, high.shape[1]), BF16)
     along = (((1,), (1,)), ((), ()))
     totals = lax.dot_general(ones, high, along, preferred_element_type=F32) + lax.dot_general(ones, low, along, preferred_element_type=F32)
     send_sums[...] = totals[0:1, :]
-    for d in range(parts):
-        send_wide[d] = wide_h[d * channels : (d + 1) * channels, :]
     for k in range(1, across):
-        push(send_sums, line_sums.at[z], 6, plane[0] + ((z + k) % across) * CORES)
-    keep(send_sums, line_sums.at[z], 6)
-
-    def send_last(d):
-        push(send_out.at[1, d], got_ref.at[1, me], 4, d)
-        push(send_wide.at[d], got_wide_ref.at[me], 5, d)
-
-    each_peer(send_last)
-    keep(send_out.at[1, me], got_ref.at[1, me], 4)
-    keep(send_wide.at[me], got_wide_ref.at[me], 5)
-    wait_bytes(line_sums, recv_sems.at[6])
+        push(send_sums, line_sums.at[z], 7, plane[0] + ((z + k) % across) * CORES)
+    keep(send_sums, line_sums.at[z], 7)
+    send_back(1)
+    wait_bytes(line_sums, recv_sems.at[7])
     for base in plane[1:]:
-        push(line_sums, got_sums_ref.at[plane_index], 7, base + z * CORES)
-    keep(line_sums, got_sums_ref.at[plane_index], 7)
-    for n, ref in enumerate((recv_h, recv_a.at[0], recv_a.at[1], got_ref.at[0], got_ref.at[1], got_wide_ref, line_sums, got_sums_ref)):
+        push(line_sums, got_sums_ref.at[plane_index], 8, base + z * CORES)
+    keep(line_sums, got_sums_ref.at[plane_index], 8)
+    for n, ref in enumerate((recv_h, recv_a.at[0], recv_a.at[1], got_ref.at[0], got_ref.at[1], got_wide_ref.at[0], got_wide_ref.at[1], line_sums, got_sums_ref)):
         sent = ref.at[pl.ds(0, ref.shape[0] - 1)]
         wait_bytes(sent, send_sems.at[n])
-    for n, ref in ((3, got_ref.at[0]), (4, got_ref.at[1]), (5, got_wide_ref), (7, got_sums_ref)):
+    for n, ref in ((3, got_ref.at[0]), (4, got_ref.at[1]), (5, got_wide_ref.at[0]), (6, got_wide_ref.at[1]), (8, got_sums_ref)):
         wait_bytes(ref, recv_sems.at[n])
 
 
@@ -288,7 +293,8 @@
         copies[-1].start()
 
     for d in range(parts):
-        wide_h[d * channels : (d + 1) * channels, :] = got_wide_ref[d]
+        for b in range(2):
+            wide_h[d * channels + b * batch : d * channels + (b + 1) * batch, :] = got_wide_ref[b, d]
         at = d // (CORES * across) * CORES + d % CORES
         sums[d : d + 1, :] = got_sums_ref[at, (d // CORES) % across]
     blocks = [wide_h[pl.ds(c, parts, stride=channels), :] for c in range(channels)]
@@ -324,7 +330,7 @@
         lambda *refs: exchange_kernel(parts, channels, across, *refs),
         out_shape=(
             pltpu.VMEM(both, BF16),
-            pltpu.VMEM((parts, channels, rows), F32),
+            pltpu.VMEM((2, parts, 2, rows), F32),
             pltpu.VMEM((planes, across, 1, rows), F32),
         ),
         in_specs=[hbm] * 11,
@@ -341,12 +347,12 @@
             pltpu.VMEM(both, BF16),
             pltpu.VMEM((parts, channels, rows), BF16),
             pltpu.VMEM(both, BF16),
-            pltpu.VMEM((parts, channels, rows), F32),
+            pltpu.VMEM((2, parts, 2, rows), F32),
             pltpu.VMEM((1, rows), F32),
             pltpu.VMEM((across, 1, rows), F32),
             pltpu.SemaphoreType.DMA((11,)),
-            pltpu.SemaphoreType.DMA((8,)),
-            pltpu.SemaphoreType.DMA((8,)),
+            pltpu.SemaphoreType.DMA((9,)),
+            pltpu.SemaphoreType.DMA((9,)),
         ],
         compiler_params=pltpu.CompilerParams(collective_id=0, has_side_effects=True),
         name="exchange_and_layer",

time: 54.9 us -> 56.2 us (1.024)
  Pallas kernels: 54.1 us -> 55.4 us
    pallas_call x1, Pallas kernels: 53.1 us -> 54.3 us  [local(): pl.pallas_call(lambda *refs: exchange_kernel(parts, channels, across, *re...]
where the time goes in v7:
time: 56.2 us; the launch traced here: 56 us
  Pallas kernels  55.4 us (99%)
  between operations  0.64 us (1%)
    pallas_call x1, Pallas kernels, local(): pl.pallas_call(lambda *refs: exchange_kernel(parts, channels, across, *re...  54.3 us

profile of v7, /device:TPU:1, one launch (start us, length us, event | category | flops | bytes accessed | tf_op | source)
XLA Modules:
  0.0 56.0 jit_solution(8461176927101102092)
XLA Ops:
  0.6 54.3 %exchange_and_layer.1 = (bf16[2,64,8,128]{3,2,1,0:T(8,128)(2,1)S(1)}, f32[2,64,2,128]{3,2,1,0:T(2,128)S(1)}, f32[8,8,1,128]{3,2,1,0:T(1,128)S(1)}) custom-call(bf16[128,256]{1,0:T(8,128)(2,1)} %refs_0_.1, bf16[128,256]{1,0:T(8,128)(2,1)} %refs_1_.1, bf16[128,256]{1,0:T(8,128)(2,1)} %refs_2_.1, bf16[128,256]{1,0:T(8,128)(2,1)} %refs_3_.1, ...), custom_call_target="tpu_custom_call" | custom-call | tf_op jit(solution)/shard_map/exchange_and_layer/pallas_call | solution.py:329
  55.0 1.0 %finish.1 = (bf16[128,256]{1,0:T(8,128)(2,1)}, bf16[128,256]{1,0:T(8,128)(2,1)}, bf16[128,256]{1,0:T(8,128)(2,1)}, bf16[128,256]{1,0:T(8,128)(2,1)}, f32[128,256]{1,0:T(8,128)}, /*index=5*/f32[3,3,256]{2,1,0:T(4,128)}) custom-call(bf16[2,64,8,128]{3,2,1,0:T(8,128)(2,1)S(1)} %get-tuple-element.9.refs_0_, f32[2,64,2,128]{3,2,1,0:T(2,128)S(1)} %get-tuple-element.10.refs_1_, ...), custom_call_target="tpu_custom_call" | custom-call | tf_op jit(solution)/shard_map/finish/pallas_call | solution.py:362

commit v8 on v7

--- a/solution.py
+++ b/solution.py
@@ -148,14 +148,10 @@
     plane = [((x + j) % far) * (CORES * across) + (core + k) % CORES for j in range(far) for k in range(CORES)]
     plane_index = x * CORES + core
 
-    skewed = lax.axis_index("tp") % 2 == 0
-
-    def each_peer(visit, early_first=False):
+    def each_peer(visit):
         def turn(step, carry):
             shift = across // 2 + (1 - 2 * (step % 2)) * ((step + 1) // 2)
             row = (z + shift) % across
-            if early_first:
-                row = jnp.where(skewed, jnp.where(step < z, step, step + 1), row)
             for base in reversed(plane):
                 visit(base + row * CORES)
             return carry
@@ -255,7 +251,7 @@
             push(send_out.at[b, d], got_ref.at[b, me], 3 + b, d)
             push(send_wide.at[b, d], got_wide_ref.at[b, me], 5 + b, d)
 
-        each_peer(visit, True)
+        each_peer(visit)
         keep(send_out.at[b, me], got_ref.at[b, me], 3 + b)
         keep(send_wide.at[b, me], got_wide_ref.at[b, me], 5 + b)
 

time: 56.2 us -> 56.2 us (level)
  no operation moved by 1% of the time
where the time goes in v8:
time: 56.2 us; the launch traced here: 56 us
  Pallas kernels  55.4 us (99%)
  between operations  0.64 us (1%)
    pallas_call x1, Pallas kernels, local(): pl.pallas_call(lambda *refs: exchange_kernel(parts, channels, across, *re...  54.3 us

profile of v8, /device:TPU:1, one launch (start us, length us, event | category | flops | bytes accessed | tf_op | source)
XLA Modules:
  0.0 56.0 jit_solution(299350622272726100)
XLA Ops:
  0.6 54.3 %exchange_and_layer.1 = (bf16[2,64,8,128]{3,2,1,0:T(8,128)(2,1)S(1)}, f32[2,64,2,128]{3,2,1,0:T(2,128)S(1)}, f32[8,8,1,128]{3,2,1,0:T(1,128)S(1)}) custom-call(bf16[128,256]{1,0:T(8,128)(2,1)} %refs_0_.1, bf16[128,256]{1,0:T(8,128)(2,1)} %refs_1_.1, bf16[128,256]{1,0:T(8,128)(2,1)} %refs_2_.1, bf16[128,256]{1,0:T(8,128)(2,1)} %refs_3_.1, ...), custom_call_target="tpu_custom_call" | custom-call | tf_op jit(solution)/shard_map/exchange_and_layer/pallas_call | solution.py:325
  55.0 1.0 %finish.1 = (bf16[128,256]{1,0:T(8,128)(2,1)}, bf16[128,256]{1,0:T(8,128)(2,1)}, bf16[128,256]{1,0:T(8,128)(2,1)}, bf16[128,256]{1,0:T(8,128)(2,1)}, f32[128,256]{1,0:T(8,128)}, /*index=5*/f32[3,3,256]{2,1,0:T(4,128)}) custom-call(bf16[2,64,8,128]{3,2,1,0:T(8,128)(2,1)S(1)} %get-tuple-element.9.refs_0_, f32[2,64,2,128]{3,2,1,0:T(2,128)S(1)} %get-tuple-element.10.refs_1_, ...), custom_call_target="tpu_custom_call" | custom-call | tf_op jit(solution)/shard_map/finish/pallas_call | solution.py:358
